TPU v7x, 128 devices: a whole 4x4x4 slice. The times are simulated.
128 devices in a mesh: map: 32 (over y, x, core), row: 4 (over z).
Axes of the slice: x: 4, y: 4, z: 4, core: 2. Of those that a mesh axis runs over, the one named last changes fastest.
Arguments:
- block_list: int32 [1024, 3], P(('map', 'row')), may hold values from 0 to 47, as said below
- block_values: bfloat16 [1024, 6, 6, 128], P(('map', 'row')), may hold values from -1.25 to 1.25
- atom_offsets: int32 [32], replicated, may hold values from 0 to 186, as said below
- density: bfloat16 [192, 192], P('row'), may hold values from -2.5 to 2.5
- metric_inverse: bfloat16 [6144, 6144], P('map', 'row'), may hold values from -0.078125 to 0.078125
Outputs:
- exchange_matrix: float32 [192, 192], P('map', 'row')
Inputs may be any that keep to these rules, and one draw needn't show every extreme that they name: `block_list`: each row is (mu atom, lambda atom, auxiliary block); no row appears twice. The 8 rows of the device at index r of row name auxiliary blocks r * 12 to (r + 1) * 12 - 1. atom_offsets is 6 times a permutation of the atoms: the atoms' functions tile 0 to 191.
All inputs are finite; a program needn't handle non-finite values.
Results may differ from a plain program's by a relative error of at most 0.0085.
Values may be sent and summed in bfloat16 or wider, within the bound.
A program may use at most 128 MiB of HBM per device.

v0:
```python
import jax
import jax.numpy as jnp
from jax import lax
from jax.sharding import PartitionSpec as P


def block_partials(triples, values, full_density, atom_slots):
    atom_count = atom_slots.shape[0]
    atom_basis = values.shape[1]
    orbitals = full_density.shape[1]
    rows_needed = jnp.take(
        full_density.reshape(atom_count, atom_basis, orbitals),
        jnp.take(atom_slots, triples[:, 1]),
        axis=0,
    )
    return jnp.einsum(
        "bijc,bjn->binc", values, rows_needed, preferred_element_type=jnp.float32
    ).astype(jnp.bfloat16)


def gather_into_half(partials, triples, atom_slots, block_count):
    atom_count = atom_slots.shape[0]
    atom_basis = partials.shape[1]
    nu_count = partials.shape[2]
    aux_width = partials.shape[3]
    segment_key = jnp.take(atom_slots, triples[:, 0]) * block_count + triples[:, 2] % block_count
    summed = jax.ops.segment_sum(
        partials.astype(jnp.float32), segment_key, atom_count * block_count
    )
    summed = summed.reshape(atom_count, block_count, atom_basis, nu_count, aux_width).transpose(
        0, 2, 3, 1, 4
    )
    return summed.reshape(atom_count * atom_basis * nu_count, block_count * aux_width).astype(
        jnp.bfloat16
    )


def tensor_for_owner(
    triples, values, atom_offsets, atom_slots, nu_local, quarter, owner_map, owner_row
):
    atom_count = atom_slots.shape[0]
    atom_basis = values.shape[1]
    aux_width = values.shape[3]
    atoms_local = nu_local // atom_basis
    lambda_offset = jnp.take(atom_offsets, triples[:, 1])
    local_atom = lambda_offset % nu_local // atom_basis
    kept_mask = (lambda_offset // nu_local == owner_map) & (triples[:, 2] // quarter == owner_row)
    segment_key = (
        jnp.take(atom_slots, triples[:, 0]) * atoms_local + local_atom
    ) * quarter + triples[:, 2] % quarter
    chosen = jnp.where(kept_mask[:, None, None, None], values, jnp.zeros_like(values))
    placed = jax.ops.segment_sum(chosen, segment_key, atom_count * atoms_local * quarter)
    placed = placed.reshape(
        atom_count, atoms_local, quarter, atom_basis, atom_basis, aux_width
    ).transpose(0, 3, 1, 4, 2, 5)
    return placed.reshape(atom_count * atom_basis, nu_local * quarter * aux_width)


def body(block_list, block_values, atom_offsets, density, metric_inverse):
    map_size = lax.axis_size("map")
    map_index = lax.axis_index("map")
    row_index = lax.axis_index("row")
    atom_count = atom_offsets.shape[0]
    atom_basis = block_values.shape[1]
    aux_width = block_values.shape[3]
    local_aux = metric_inverse.shape[1]
    quarter = local_aux // aux_width
    orbitals = atom_count * atom_basis
    nu_local = orbitals // map_size
    atom_slots = atom_offsets // atom_basis
    full_density = lax.all_gather(density, "row", axis=0, tiled=True)
    triples = lax.all_gather(block_list, "map", axis=0, tiled=True)
    values = lax.all_gather(block_values, "map", axis=0, tiled=True)
    own_partials = block_partials(block_list, block_values, full_density, atom_slots)
    partials = lax.all_to_all(own_partials, "map", split_axis=2, concat_axis=0, tiled=True)
    own_half = gather_into_half(partials, triples, atom_slots, quarter)
    half_tensor = lax.all_gather(own_half, "row", axis=1, tiled=True)
    fitted_sum = jnp.dot(
        half_tensor,
        lax.all_gather(metric_inverse, "map", axis=0, tiled=True),
        preferred_element_type=jnp.float32,
    )
    fitted = fitted_sum.astype(jnp.bfloat16).reshape(orbitals, nu_local * local_aux)
    tensor_slice = tensor_for_owner(
        triples, values, atom_offsets, atom_slots, nu_local, quarter, map_index, row_index
    )
    partial_exchange = lax.dot_general(
        fitted, tensor_slice, (((1,), (1,)), ((), ())), preferred_element_type=jnp.float32
    )
    by_column = lax.psum_scatter(partial_exchange, "row", scatter_dimension=1, tiled=True)
    return lax.psum_scatter(by_column, "map", scatter_dimension=0, tiled=True)


def solution(mesh):
    placed = (
        P(("map", "row"), None),
        P(("map", "row"), None, None, None),
        P(),
        P("row", None),
        P("map", "row"),
    )
    return jax.shard_map(
        body, mesh=mesh, in_specs=placed, out_specs=P("map", "row"), check_vma=False
    )
```

profile of v0, /device:TPU:1, one launch (start us, length us, event | category | flops | bytes accessed | tf_op | source)
XLA Modules:
  0.0 590.3 jit_solution(4406480883751726572)
XLA Ops:
  6.5 0.7 all-gather.9.cloned.1.call-update
  7.3 11.7 %all_gather.16 = bf16[192,192]{1,0:T(8,128)(2,1)S(1)} all-gather(bf16[48,192]{1,0:T(8,128)(2,1)} %param.10), channel_id=1, replica_groups=mesh['map'=32,'row'=4] {'row'}, dimensions={0}, use_global_device_ids=true | all-gather | bytes 92160 | tf_op jit(solution)/shard_map/all_gather | solution.py:71
  19.0 0.7 fusion.6
  19.7 0.7 and_select_fusion.8
  20.3 0.6 gather_fusion
  21.0 0.7 and_bitcast_fusion
  21.7 0.6 gather_fusion.1
  22.2 2.1 convert_bitcast_fusion.1
  24.3 2.9 copy.49
  27.3 10.3 %all-to-all-start = ((bf16[8,6,192,128]{3,0,1,2:T(8,128)(2,1)}), bf16[8,6,192,128]{3,0,1,2:T(8,128)(2,1)S(1)}, u32[]{:S(2)}, u32[]{:S(2)}) async-start(bf16[8,6,192,128]{3,0,1,2:T(8,128)(2,1)} %copy.49), calls=%async_computation | async-start | bytes 4718592 | tf_op jit(solution)/shard_map/all_to_all | solution.py:75
  37.5 0.0 all-gather.5.cloned.1.call-start
  37.6 49.3 %all-gather = s32[32,8,3]{1,2,0:T(4,128)S(1)} all-gather(s32[1,8,3]{1,2,0:T(4,128)S(1)} %bitcast.130), channel_id=1, replica_groups=mesh['map'=32,'row'=4] {'map'}, dimensions={0}, use_global_device_ids=true | all-gather | bytes 3168 | tf_op jit(solution)/shard_map/all_gather | solution.py:72
  86.9 0.1 reshape.164
  87.1 0.7 fusion.11
  87.7 0.7 fusion.9
  88.5 0.7 fusion.10
  89.2 0.7 fusion.8
  90.0 19.7 %compare_and_fusion = (pred[256]{0:T(512)(128)(4,1)S(1)}, s32[256]{0:T(256)S(1)}) fusion(s32[256]{0:T(256)S(1)} %bitcast.127, pred[256]{0:T(512)(128)(4,1)S(1)} %compare_reduce_fusion, s32[256]{0:T(256)S(1)} %bitcast.124, s32[]{:T(128)S(6)} %axis_index.25, s32[]{:T(128)S(6)} %axis_index.23, s32[]{:T(128)} %bitcast.78, s32[]{:T(128)} %bitcast.77, ...), kind=kLoop, calls=%fused_computation.88 | loop fusion | flops 21504 | bytes 4744 | tf_op jit(solution)/shard_map/and | solution.py:47
  109.6 20.1 %multiply_add_fusion = (s32[256]{0:T(256)S(1)}, s32[256]{0:T(256)S(1)}) fusion(s32[256]{0:T(256)S(1)} %get-tuple-element.7, s32[256]{0:T(256)S(1)} %bitcast.125, s32[]{:T(128)} %bitcast.33, s32[]{:T(128)} %bitcast.32, s32[]{:T(128)} %bitcast.31, s32[]{:T(128)} %bitcast.30, s32[]{:T(128)} %bitcast.29, s32[]{:T(128)} %bitcast.28, s32[]{:T(128)} %bitcast.27, ...), kind=kLoop, calls=%fused_computation.97 | loop fusion | flops 23296 | bytes 5248 | tf_op jit(solution)/shard_map/add | solution.py:48
  129.7 0.4 copy.50
  130.2 0.6 copy_bitcast_fusion.1
  130.7 5.5 copy.52
  136.2 4.2 broadcast_in_dim.42
  140.5 36.5 %scatter_fusion = f32[384,6,6,128]{3,2,1,0:T(8,128)} fusion(f32[384,6,6,128]{3,2,1,0:T(8,128)} %broadcast_in_dim.42, s32[256]{0:T(256)S(1)} %multiply_add_fusion.1, f32[256,6,6,128]{3,2,1,0:T(8,128)} %copy.52), kind=kCustom, calls=%fused_computation.2 | custom fusion | flops 1179648 | bytes 14156800 | tf_op jit(solution)/shard_map/scatter-add | solution.py:27
  177.0 6.0 %copy.68 = bf16[384,6,6,128]{3,0,2,1:T(8,128)(2,1)S(1)} copy(f32[384,6,6,128]{3,2,1,0:T(8,128)} %scatter_fusion) | data formatting | bytes 10616832 | tf_op jit(solution)/shard_map/scatter-add | solution.py:27
  182.9 3.3 convert_element_type.40
  186.3 3.7 copy.54
  190.0 3.5 copy.70
  193.5 0.0 all-gather.7.cloned.1.call-start
  193.6 0.7 all-gather.7.cloned.1.call-update
  194.3 0.3 reduce-scatter.3.cloned.1.call-start
  194.5 0.0 all-gather.9.cloned.1.call-done
  194.5 1.9 broadcast_select_fusion
  196.5 1.6 copy.55
  198.1 2.8 broadcast_in_dim.46
  200.9 33.5 %scatter_fusion.1 = bf16[384,6,6,128]{3,2,1,0:T(8,128)(2,1)} fusion(bf16[384,6,6,128]{3,2,1,0:T(8,128)(2,1)} %broadcast_in_dim.46, s32[256]{0:T(256)S(1)} %get-tuple-element.8, bf16[256,6,6,128]{3,2,1,0:T(8,128)(2,1)S(1)} %copy.55), kind=kCustom, calls=%fused_computation.3 | custom fusion | flops 1179648 | bytes 7078912 | tf_op jit(solution)/shard_map/scatter-add | solution.py:52
  234.3 6.1 %copy.69 = bf16[32,1,12,6,6,128]{5,2,4,3,0,1:T(8,128)(2,1)} copy(bf16[32,1,12,6,6,128]{5,4,3,2,0,1:T(8,128)(2,1)} %bitcast.118) | data formatting | bytes 7077888 | tf_op jit(solution)/shard_map/reshape | solution.py:53
  240.4 6.6 %reshape.46 = bf16[192,9216]{1,0:T(8,128)(2,1)} reshape(bf16[32,6,1,6,12,128]{5,4,3,1,0,2:T(8,128)(2,1)} %bitcast.121) | data formatting | bytes 7077888 | tf_op jit(solution)/shard_map/reshape | solution.py:56
  247.1 77.2 %all-gather.5.cloned.1.call-done = bf16[1152,6144]{1,0:T(8,128)(2,1)} async-done(((bf16[1152,1536]{1,0:T(8,128)(2,1)}), bf16[1152,6144]{1,0:T(8,128)(2,1)}) %all-gather.5.cloned.1.call-update) | async-done | bytes 14155792 | tf_op jit(solution)/shard_map/all_gather | solution.py:77
  324.2 81.1 %all-gather.7.cloned.1.call-done = bf16[6144,1536]{1,0:T(8,128)(2,1)} async-done(((bf16[192,1536]{1,0:T(8,128)(2,1)}), bf16[6144,1536]{1,0:T(8,128)(2,1)}) %all-gather.7.cloned.1.call-update) | async-done | bytes 18874384 | tf_op jit(solution)/shard_map/all_gather | solution.py:80
  405.4 26.6 %convolution_convert_fusion = bf16[1152,1536]{1,0:T(8,128)(2,1)S(1)} fusion(bf16[1152,6144]{1,0:T(8,128)(2,1)} %all-gather.5.cloned.1.call-done, bf16[6144,1536]{1,0:T(8,128)(2,1)} %all-gather.7.cloned.1.call-done), kind=kOutput, calls=%fused_computation.4 | convolution fusion | flops 21745041408 | bytes 36569088 | tf_op jit(solution)/shard_map/dot_general | solution.py:78
  432.0 5.3 reshape.44
  437.3 4.9 fusion.12
  442.2 0.6 dynamic-slice
  443.4 16.5 %reduce-scatter.3.cloned.1.call-done = f32[192,48]{0,1:T(8,128)} async-done(((f32[192,192]{0,1:T(8,128)}), f32[192,48]{0,1:T(8,128)}) %reduce-scatter.3.cloned.1.call-update) | async-done | bytes 36880 | tf_op jit(solution)/shard_map/reduce_scatter | solution.py:90
  459.9 123.1 %all-reduce = f32[192,48]{0,1:T(8,128)S(1)} all-reduce(f32[192,48]{0,1:T(8,128)} %reduce-scatter.3.cloned.1.call-done), channel_id=3, replica_groups=mesh['map'=32,'row'=4] {'map'}, use_global_device_ids=true, to_apply=%region_3.5.clone | all-reduce | flops 9216 | bytes 73728
  583.1 0.1 constant_dynamic-slice_fusion
  583.1 0.7 copy.57
  (17 shorter events, 0.2 us)
Async XLA Ops:
  6.5 188.0 %all-gather.9.cloned.1.call-start = ((), (), s32[]{:S(2)}) async-start(), calls=%async_computation.4 | async-start | bytes 2433024 | tf_op jit(solution)/shard_map/all_gather | solution.py:73
  24.3 13.3 %copy-start.1 = (s32[8,3]{0,1:T(4,128)S(1)}, s32[8,3]{0,1:T(4,128)}, u32[]{:S(2)}) copy-start(s32[8,3]{0,1:T(4,128)} %param.7) | copy-start | bytes 292
  24.3 62.7 %copy-start = (s32[32]{0:T(128)S(1)}, s32[32]{0:T(128)}, u32[]{:S(2)}) copy-start(s32[32]{0:T(128)} %param.9) | copy-start | bytes 388
  27.3 102.5 %all-to-all-start = ((bf16[8,6,192,128]{3,0,1,2:T(8,128)(2,1)}), bf16[8,6,192,128]{3,0,1,2:T(8,128)(2,1)S(1)}, u32[]{:S(2)}, u32[]{:S(2)}) async-start(bf16[8,6,192,128]{3,0,1,2:T(8,128)(2,1)} %copy.49), calls=%async_computation | async-start | bytes 4718592 | tf_op jit(solution)/shard_map/all_to_all | solution.py:75
  37.5 286.7 %all-gather.5.cloned.1.call-start = ((), (), s32[]{:S(2)}) async-start(), calls=%async_computation.2 | async-start | bytes 17694720 | tf_op jit(solution)/shard_map/all_gather | solution.py:77
  193.5 211.9 %all-gather.7.cloned.1.call-start = ((), (), s32[]{:S(2)}) async-start(), calls=%async_computation.3 | async-start | bytes 19464192 | tf_op jit(solution)/shard_map/all_gather | solution.py:80
  194.3 265.7 %reduce-scatter.3.cloned.1.call-start = ((), (), s32[]{:S(2)}) async-start(), calls=%async_computation.5 | async-start | bytes 245760 | tf_op jit(solution)/shard_map/reduce_scatter | solution.py:90
  437.3 4.9 copy-start.2
Sparse Core Ops, SparseCore 0:
  9.5 66.5 all-gather.8
  193.6 130.5 all-gather.4
  326.5 78.8 all-gather.6
  442.3 17.5 reduce-scatter.2
where the time goes:
time: 597 us; the launch traced here: 590 us
  blocking collectives  184 us (31%)
  waiting for transfers between devices  176 us (29%)
  other arithmetic  114 us (19%)
  local copies, waits for them, and re-layouts  57.7 us (10%)
  matrix products  33.5 us (6%)
  between operations  14 us (2%)
  starting transfers between devices  10.6 us (2%)
    unnamed x1, blocking collectives  123 us
    all_gather x1, waiting for transfers between devices, body(): lax.all_gather(metric_inverse, 'map', axis=0, tiled=True)  81.1 us
    all_gather x1, waiting for transfers between devices, body(): half_tensor = lax.all_gather(own_half, 'row', axis=1, tiled=True)  77.2 us
    all_gather x1, blocking collectives, body(): triples = lax.all_gather(block_list, 'map', axis=0, tiled=True)  49.3 us
    scatter-add x1, other arithmetic, gather_into_half(): jax.ops.segment_sum(partials.astype(jnp.float32), segment_key, atom_count...  36.5 us
    scatter-add x1, other arithmetic, tensor_for_owner(): jax.ops.segment_sum(chosen, segment_key, atom_count * atoms_local * quarter)  33.5 us
    dot_general x1, matrix products, body(): jnp.dot(half_tensor, lax.all_gather(metric_inverse, 'map', axis=0, tiled=...  26.6 us
    add x1, other arithmetic, tensor_for_owner(): (jnp.take(atom_slots, triples[:, 0]) * atoms_local + local_atom) * quarter  20.1 us
  transfers between devices with their start and end apart: 5, of which 3 were waited for; matrix products, arithmetic and copies ran while one was open for 28% of the time, Pallas kernels for 0%

commit v1 on v0

v1 whole, which is shorter than its diff:
```python
import jax
import jax.numpy as jnp
from jax import lax
from jax.experimental import pallas as pl
from jax.experimental.pallas import tpu as pltpu
from jax.sharding import PartitionSpec as P

HI = lax.Precision.HIGHEST
F32, BF16, I32 = jnp.float32, jnp.bfloat16, jnp.int32
NT = (((1,), (1,)), ((), ()))
GROUP = 32
CHUNK = 16
UNROLL = 8


def iota(shape, axis):
    return lax.broadcasted_iota(I32, shape, axis)


def contract_kernel(codeq, codep, meta, bq, bp, v, dt, out, vp, xbuf, hbuf, dexp, rbuf, ebuf, kbuf):
    parity = meta[35]
    vp[...] = jnp.zeros_like(vp)
    vp[pl.ds(pl.multiple_of(parity * 64, 64), 192), :] = v[...]
    r48, c36 = iota((48, 36), 0), iota((48, 36), 1)
    spread = ((c36 // 6 == r48 % 8) & (c36 % 6 == r48 // 8)).astype(F32).astype(BF16)

    def x_step(step, carry):
        for u in range(UNROLL):
            t = step * UNROLL + u
            code = codeq[t]
            k = code & 255
            q = (code >> 8) & 15
            padded = jnp.dot(spread, bq[k], preferred_element_type=F32).astype(BF16)
            w = vp[:, pl.ds(pl.multiple_of(q * 128, 128), 128)]
            x = lax.dot_general(padded, w, NT, preferred_element_type=F32)
            for j in range(6):
                xbuf[j, t] = x[8 * j:8 * j + 8, :]
        return carry

    lax.fori_loop(0, 256 // UNROLL, x_step, 0)
    kbuf[...] = jnp.zeros_like(kbuf)

    mask = (iota((8, 128), 1) // 6 == iota((8, 128), 0)) & (iota((8, 128), 0) < 6)
    lam, lane = iota((192, 128), 0), iota((192, 128), 1)
    lane_j = lane % 6

    def group(e, base, cnt):
        ebuf[...] = jnp.zeros_like(ebuf)
        rbuf[...] = jnp.zeros_like(rbuf)

        def h_step(t, carry):
            code = codep[base + t]
            k = code & 255
            l = (code >> 8) & 31
            a = (code >> 13) & 31
            sel = (lam == 6 * l + lane_j).astype(F32).astype(BF16)
            dexp[...] = jnp.dot(dt[...], sel, preferred_element_type=F32)
            b = bp[k]
            for c in range(6):
                d = dexp[32 * c:32 * c + 32, :]
                w = jnp.where(mask[None], d[:, None, :], 0.0).reshape(256, 128).astype(BF16)
                h = jnp.dot(w[:, :36], b, preferred_element_type=F32)
                hbuf[32 * c:32 * c + 32, t] = h.reshape(32, 8, 128)
            row, col = iota((8, 256), 0), iota((8, 256), 1)
            ebuf[pl.ds(pl.multiple_of(8 * t, 8), 8), :] = ((col == 6 * a + row) & (row < 6)).astype(F32)
            return carry

        lax.fori_loop(0, cnt, h_step, 0)

        def n_step(n, carry):
            s0, s1 = meta[n], meta[n + 1]

            def c_step(c, carry):
                k0 = s0 + CHUNK * c
                xs, hs = [], []
                for j in range(6):
                    xs.append(xbuf[j, pl.ds(k0, CHUNK), :, pl.ds(pl.multiple_of(e * 128, 128), 128)].reshape(CHUNK * 8, 128).astype(BF16))
                    hs.append(hbuf[n * 6 + j].reshape(GROUP * 8, 128).astype(BF16))
                o = lax.dot_general(jnp.concatenate(xs, axis=1), jnp.concatenate(hs, axis=1), NT, preferred_element_type=F32)
                for t in range(CHUNK):
                    s = jnp.where(k0 + t < s1, (codeq[k0 + t] >> 12) & 31, 32)
                    at = pl.ds(pl.multiple_of(8 * s, 8), 8)
                    rbuf[at, :] += o[8 * t:8 * t + 8, :]
                return carry

            return lax.fori_loop(0, (s1 - s0 + CHUNK - 1) // CHUNK, c_step, carry)

        lax.fori_loop(0, 32, n_step, 0)
        r = jnp.where(iota((256, 256), 1) < 8 * cnt, rbuf[0:256, :], 0.0)
        kbuf[...] += jnp.dot(r, ebuf[...], preferred_element_type=F32, precision=HI)

    n0, n1 = meta[33], meta[34]

    def g_step(g, carry):
        g0 = (n0 + GROUP - 1) // GROUP
        e = (g >= g0).astype(I32)
        first = jnp.where(e == 1, n0, 0)
        left = jnp.where(e == 1, n1, n0) - GROUP * (g - e * g0)
        group(e, first + GROUP * (g - e * g0), jnp.minimum(left, GROUP))
        return carry

    lax.fori_loop(0, (n0 + GROUP - 1) // GROUP + (n1 + GROUP - 1) // GROUP, g_step, 0)
    r, c = iota((256, 192), 0), iota((256, 192), 1)
    squeeze = ((r // 8 == c // 6) & (r % 8 == c % 6)).astype(F32)
    out[...] = jnp.dot(kbuf[...].T, squeeze, preferred_element_type=F32, precision=HI)[:192, :]


def contract(codeq, codep, meta, bq, bp, v, dt):
    smem = pl.BlockSpec(memory_space=pltpu.SMEM)
    vmem = pl.BlockSpec(memory_space=pltpu.VMEM)
    return pl.pallas_call(
        contract_kernel,
        out_shape=jax.ShapeDtypeStruct((192, 192), F32),
        in_specs=[smem] * 3 + [vmem] * 4,
        out_specs=vmem,
        scratch_shapes=[
            pltpu.VMEM((256, 1536), BF16),
            pltpu.VMEM((6, 256 + CHUNK, 8, 256), F32),
            pltpu.VMEM((192, GROUP, 8, 128), F32),
            pltpu.VMEM((192, 128), F32),
            pltpu.VMEM((264, 256), F32),
            pltpu.VMEM((256, 256), F32),
            pltpu.VMEM((256, 256), F32),
        ],
        compiler_params=pltpu.CompilerParams(vmem_limit_bytes=60 << 20),
        name="contract",
    )(codeq, codep, meta, bq, bp, v, dt)


def ranks(key):
    n = key.shape[-1]
    mine, other = key[..., :, None], key[..., None, :]
    at = jnp.arange(n, dtype=I32)
    before = (other < mine) | ((other == mine) & (at[None, :] < at[:, None]))
    return jnp.sum(before.astype(I32), axis=-1)


def tables(listq, listp, slots, first_block, row_start):
    def slot(x):
        return jnp.sum(jnp.where(x[:, None] == jnp.arange(32, dtype=I32), slots, 0), axis=1)
    at = jnp.arange(256, dtype=I32)
    keyq = slot(listq[:, 1])
    codeq = at + ((listq[:, 2] - row_start) << 8) + (slot(listq[:, 0]) << 12)
    p = listp[:, 2] - first_block
    keyp = jnp.where((p == 0) | (p == 1), p, 2)
    codep = at + (slot(listp[:, 1]) << 8) + (slot(listp[:, 0]) << 13)
    key = jnp.stack([keyq, keyp])
    code = jnp.stack([codeq, codep])
    rank = ranks(key)
    ordered = jnp.sum(jnp.where(rank[:, None, :] == at[None, :, None], code[:, None, :], 0), axis=2)
    starts = jnp.sum((keyq[None, :] < jnp.arange(33, dtype=I32)[:, None]).astype(I32), axis=1)
    counts = jnp.sum((keyp[None, :] == jnp.arange(2, dtype=I32)[:, None]).astype(I32), axis=1)
    return jnp.pad(ordered[0], (0, CHUNK)), ordered[1], starts, counts


def body(block_list, block_values, atom_offsets, density, metric_inverse):
    m, r = lax.axis_index("map"), lax.axis_index("row")
    row = m // 8
    lists = lax.all_gather(block_list, ("map", "row"), axis=0).reshape(32, 4, 8, 3)
    values = lax.all_gather(block_values.reshape(8, 36, 128), ("map", "row"), axis=0).reshape(32, 4, 8, 36, 128)
    full = lax.all_gather(density, "row", axis=0, tiled=True)

    def pick(x, at):
        return lax.dynamic_index_in_dim(x, at, 1, keepdims=False).reshape((256,) + x.shape[3:])
    parity = m % 2
    codeq, codep, starts, counts = tables(pick(lists, r), pick(lists, row), atom_offsets // 6, 3 * (m // 2) + parity, r * 12)
    meta = jnp.concatenate([starts, counts, jnp.stack([parity, parity, parity, parity, parity]).astype(I32)])
    part = contract(codeq, codep, meta, pick(values, r), pick(values, row), metric_inverse, full.T)
    by_column = lax.psum_scatter(part, "row", scatter_dimension=1, tiled=True)
    return lax.psum_scatter(by_column, "map", scatter_dimension=0, tiled=True)


def solution(mesh):
    placed = (
        P(("map", "row"), None),
        P(("map", "row"), None, None, None),
        P(),
        P("row", None),
        P("map", "row"),
    )
    return jax.shard_map(
        body, mesh=mesh, in_specs=placed, out_specs=P("map", "row"), check_vma=False
    )
```

time: 597 us -> 331 us (0.55)
  waiting for transfers between devices: 176 us -> 34.4 us
  other arithmetic: 114 us -> 1.53 us
  Pallas kernels: 0 us -> 67.4 us
  local copies, waits for them, and re-layouts: 57.7 us -> 13.5 us
  matrix products: 33.5 us -> 0 us
  blocking collectives: 184 us -> 196 us
  starting transfers between devices: 10.6 us -> 0.04 us
    all_gather x3 -> x1, waiting for transfers between devices: 158 us -> 0.83 us  [body(): lax.all_gather(block_values.reshape(8, 36, 128), ('map', 'row'), axis=0)]
    scatter-add x2 -> x0, other arithmetic: 69.9 us -> none  [the longest x1 36.5 us: gather_into_half(): jax.ops.segment_sum(partials.astype(jnp.float32), segment_key, atom_count...]
    pallas_call x0 -> x1, Pallas kernels: none -> 67.4 us  [contract(): pl.pallas_call(contract_kernel, out_shape=jax.ShapeDtypeStruct((192, 192)...]
    dot_general x3 -> x0, matrix products: 33.5 us -> none  [the longest x1 26.6 us: body(): jnp.dot(half_tensor, lax.all_gather(metric_inverse, 'map', axis=0, tiled=...]
    unnamed x4 -> x3, waiting for transfers between devices: 1.42 us -> 33.6 us
    add x2, other arithmetic: 20.1 us -> 0.02 us  [the longest x1 0.01 us: tables(): codeq = at + (listq[:, 2] - row_start << 8) + (slot(listq[:, 0]) << 12)]
    and x1 -> x0, other arithmetic: 19.7 us -> none  [tensor_for_owner(): (lambda_offset // nu_local == owner_map) & (triples[:, 2] // quarter == o...]
    reshape x4 -> x2, local copies, waits for them, and re-layouts: 18.1 us -> 0.19 us  [pick(): lax.dynamic_index_in_dim(x, at, 1, keepdims=False)]
  transfers between devices with their start and end apart: 5 -> 2, of which waited for: 3 -> 2; matrix products, arithmetic and copies ran while one was open for 28% -> 2% of each run, Pallas kernels for 0% -> 0%
where the time goes in v1:
time: 331 us; the launch traced here: 327 us
  blocking collectives  196 us (59%)
  Pallas kernels  67.4 us (20%)
  waiting for transfers between devices  34.4 us (10%)
  between operations  14.2 us (4%)
  local copies, waits for them, and re-layouts  13.5 us (4%)
    unnamed x1, blocking collectives  123 us
    pallas_call x1, Pallas kernels, contract(): pl.pallas_call(contract_kernel, out_shape=jax.ShapeDtypeStruct((192, 192)...  67.4 us
    all_gather x1, blocking collectives, body(): lax.all_gather(block_list, ('map', 'row'), axis=0).reshape(32, 4, 8, 3)  60.9 us
    unnamed x3, waiting for transfers between devices  33.6 us
    all_gather x1, blocking collectives, body(): full = lax.all_gather(density, 'row', axis=0, tiled=True)  11.7 us
    dynamic_slice x4, local copies, waits for them, and re-layouts, pick(): lax.dynamic_index_in_dim(x, at, 1, keepdims=False)  6.89 us
  transfers between devices with their start and end apart: 2, of which 2 were waited for; matrix products, arithmetic and copies ran while one was open for 2% of the time, Pallas kernels for 0%

profile of v1, /device:TPU:1, one launch (start us, length us, event | category | flops | bytes accessed | tf_op | source)
XLA Modules:
  0.0 326.8 jit_solution(4781538569335374759)
XLA Ops:
  6.5 0.0 all-gather.4.cloned.1.call-start
  6.5 0.7 all-gather.4.cloned.1.call-update
  7.3 0.0 reduce-scatter.4.cloned.1.call-start
  7.3 11.7 %all_gather.15 = bf16[192,192]{1,0:T(8,128)(2,1)S(1)} all-gather(bf16[48,192]{1,0:T(8,128)(2,1)} %param.8), channel_id=1, replica_groups=mesh['map'=32,'row'=4] {'row'}, dimensions={0}, use_global_device_ids=true | all-gather | bytes 92160 | tf_op jit(solution)/shard_map/all_gather | solution.py:161
  19.0 0.7 copy.21
  19.7 60.9 %all-gather.1 = s32[128,8,3]{1,2,0:T(4,128)S(1)} all-gather(s32[1,8,3]{1,2,0:T(4,128)} %bitcast.57), channel_id=2, replica_groups=mesh['map'=32,'row'=4] {'map','row'}, dimensions={0}, use_global_device_ids=true | all-gather | bytes 12384 | tf_op jit(solution)/shard_map/all_gather | solution.py:159
  80.7 0.1 reshape.132
  80.8 0.1 reshape.131
  80.9 0.7 and_select_fusion
  81.6 0.1 select_reduce_fusion.4
  81.8 0.3 convert_reduce_fusion
  82.1 0.2 select_reduce_fusion
  82.3 0.6 fusion.7
  82.9 0.6 pad.4.codeq
  83.4 0.1 fusion
  83.6 0.1 convert_reduce_fusion.1
  83.7 0.7 concatenate.3.meta
  84.4 0.8 all-gather.4.cloned.1.call-done
  85.2 2.7 constant_dynamic-slice_fusion
  87.9 2.1 copy.20
  90.0 2.1 copy.19
  92.1 0.0 copy-start
  92.1 67.4 %contract.1 = f32[192,192]{1,0:T(8,128)} custom-call(s32[272]{0:T(512)} %pad.4.codeq, s32[256]{0:T(256)} %bitcast.46, s32[40]{0:T(128)} %concatenate.3.meta, bf16[256,36,128]{2,1,0:T(8,128)(2,1)} %bitcast.39, bf16[256,36,128]{2,1,0:T(8,128)(2,1)} %bitcast.38, bf16[192,1536]{1,0:T(8,128)(2,1)} %v.1, bf16[192,192]{1,0:T(8,128)(2,1)} %bitcast.43), custom_call_target="tpu_custom_call" | custom-call | tf_op jit(solution)/shard_map/contract/pallas_call | solution.py:111
  159.4 1.7 copy.22
  161.2 0.0 reduce-scatter.4.cloned.1.call-update
  161.2 0.0 copy-done
  161.2 0.6 dynamic-slice
  162.4 32.9 %reduce-scatter.4.cloned.1.call-done = f32[48,192]{1,0:T(8,128)} async-done(((f32[192,192]{1,0:T(8,128)}), f32[48,192]{1,0:T(8,128)}) %reduce-scatter.4.cloned.1.call-update) | async-done | bytes 36880
  195.3 0.9 copy.23
  196.2 123.1 %all-reduce.1 = f32[192,48]{1,0:T(8,128)S(1)} all-reduce(f32[192,48]{1,0:T(8,128)S(1)} %copy.23), channel_id=4, replica_groups=mesh['map'=32,'row'=4] {'map'}, use_global_device_ids=true, to_apply=%region_9.10.clone | all-reduce | flops 9216 | bytes 73728
  319.3 0.6 constant_dynamic-slice_fusion.4
  (14 shorter events, 0.1 us)
Async XLA Ops:
  6.5 78.6 %all-gather.4.cloned.1.call-start = ((), (), s32[]{:S(2)}) async-start(), calls=%async_computation.1 | async-start | bytes 9510912 | tf_op jit(solution)/shard_map/all_gather | solution.py:160
  7.3 188.1 %reduce-scatter.4.cloned.1.call-start = ((), (), s32[]{:S(2)}) async-start(), calls=%async_computation.2 | async-start | bytes 245760
  92.1 69.1 %copy-start = (u32[128]{0:T(128)S(1)}, u32[128]{0:T(128)}, u32[]{:S(2)}) copy-start(u32[128]{0:T(128)} %constant.82) | copy-start | bytes 1540
Sparse Core Ops, SparseCore 0:
  10.5 74.6 all-gather.3
  161.3 33.9 reduce-scatter.3

commit v2 on v1

--- a/solution.py
+++ b/solution.py
@@ -8,6 +8,7 @@
 HI = lax.Precision.HIGHEST
 F32, BF16, I32 = jnp.float32, jnp.bfloat16, jnp.int32
 NT = (((1,), (1,)), ((), ()))
+MESH = pl.DeviceIdType.MESH
 GROUP = 32
 CHUNK = 16
 UNROLL = 8
@@ -62,7 +63,7 @@
                 h = jnp.dot(w[:, :36], b, preferred_element_type=F32)
                 hbuf[32 * c:32 * c + 32, t] = h.reshape(32, 8, 128)
             row, col = iota((8, 256), 0), iota((8, 256), 1)
-            ebuf[pl.ds(pl.multiple_of(8 * t, 8), 8), :] = ((col == 6 * a + row) & (row < 6)).astype(F32)
+            ebuf[pl.ds(pl.multiple_of(8 * t, 8), 8), :] = (col == 8 * a + row).astype(F32)
             return carry
 
         lax.fori_loop(0, cnt, h_step, 0)
@@ -100,9 +101,9 @@
         return carry
 
     lax.fori_loop(0, (n0 + GROUP - 1) // GROUP + (n1 + GROUP - 1) // GROUP, g_step, 0)
-    r, c = iota((256, 192), 0), iota((256, 192), 1)
+    r, c = iota((256, 256), 0), iota((256, 256), 1)
     squeeze = ((r // 8 == c // 6) & (r % 8 == c % 6)).astype(F32)
-    out[...] = jnp.dot(kbuf[...].T, squeeze, preferred_element_type=F32, precision=HI)[:192, :]
+    out[...] = jnp.dot(kbuf[...].T, squeeze, preferred_element_type=F32, precision=HI)
 
 
 def contract(codeq, codep, meta, bq, bp, v, dt):
@@ -110,7 +111,7 @@
     vmem = pl.BlockSpec(memory_space=pltpu.VMEM)
     return pl.pallas_call(
         contract_kernel,
-        out_shape=jax.ShapeDtypeStruct((192, 192), F32),
+        out_shape=jax.ShapeDtypeStruct((256, 256), F32),
         in_specs=[smem] * 3 + [vmem] * 4,
         out_specs=vmem,
         scratch_shapes=[
@@ -153,21 +154,226 @@
     return jnp.pad(ordered[0], (0, CHUNK)), ordered[1], starts, counts
 
 
+def place():
+    m, z = lax.axis_index("map"), lax.axis_index("row")
+    return m, (m // 2) % 4, m // 8, z, m % 2
+
+
+def at_map(x, y, c):
+    return (y * 4 + x) * 2 + c
+
+
+def greet(devices):
+    barrier = pltpu.get_barrier_semaphore()
+    for d in devices:
+        pl.semaphore_signal(barrier, inc=1, device_id=d, device_id_type=MESH)
+    pl.semaphore_wait(barrier, len(devices))
+
+
+def gather_kernel(own, dens, bq, bp, dout, stage, s_send, s_z, s_d, s_ax, s_ay, s_as, s_by, s_bx, s_bs, s_loc):
+    m, x, y, z, c = place()
+    way = 1 - 2 * c
+    o = 1 - c
+
+    def dev(xx, yy, zz, cc):
+        return (at_map(lax.rem(xx + 4, 4), lax.rem(yy + 4, 4), cc), lax.rem(zz + 4, 4))
+
+    def r4(v):
+        return lax.rem(v + 8, 4)
+
+    sib = dev(x, y, z, o)
+    greet([dev(x + 1, y, z, c), dev(x + 3, y, z, c), dev(x, y + 1, z, c), dev(x, y + 3, z, c), dev(x, y + 2, z, c), dev(x, y, z + 1, c), dev(x, y, z + 3, c), sib])
+    sends = []
+
+    def send(src, dst, recv, device):
+        n = len(sends)
+        d = pltpu.make_async_remote_copy(src_ref=src, dst_ref=dst, send_sem=s_send.at[n], recv_sem=recv, device_id=device, device_id_type=MESH)
+        d.start()
+        sends.append(d)
+
+    def arrive(dst, recv):
+        pltpu.make_async_remote_copy(src_ref=dst, dst_ref=dst, send_sem=s_send.at[0], recv_sem=recv, device_id=sib, device_id_type=MESH).wait_recv()
+
+    def slot(ref, xx, yy, cc=None):
+        return ref.at[at_map(r4(xx), r4(yy), c if cc is None else cc)]
+
+    drows = pl.ds(pl.multiple_of(z * 48, 16), 48)
+    for s in (1, 3):
+        send(own, stage.at[z], s_z.at[z], dev(x, y, z + s, c))
+        send(dens, dout.at[z], s_d.at[z], dev(x, y, z + s, c))
+    for s in (1, 3):
+        send(own, slot(bq, x, y), s_ax.at[x], dev(x + s, y, z, c))
+    for s in (1, 3):
+        send(own, slot(bq, x, y), s_ay.at[x, y], dev(x, y + s, z, c))
+    send(own, slot(bq, x, y), s_as.at[x, y], sib)
+    local = [
+        pltpu.make_async_copy(own, slot(bq, x, y), s_loc.at[0]),
+        pltpu.make_async_copy(own, stage.at[z], s_loc.at[1]),
+        pltpu.make_async_copy(dens, dout.at[z], s_loc.at[2]),
+    ]
+    for d in local:
+        d.start()
+    zf = r4(z - way)
+    arrive(stage.at[zf], s_z.at[zf])
+    send(stage.at[zf], stage.at[zf], s_z.at[zf], dev(x, y, z + way, c))
+    arrive(dout.at[zf], s_d.at[zf])
+    send(dout.at[zf], dout.at[zf], s_d.at[zf], dev(x, y, z + way, c))
+    def spread_y(xx):
+        for s in (1, 3):
+            send(slot(bq, xx, y), slot(bq, xx, y), s_ay.at[r4(xx), y], dev(x, y + s, z, c))
+        send(slot(bq, xx, y), slot(bq, xx, y), s_as.at[r4(xx), y], sib)
+
+    xf, xb = r4(x - way), r4(x + way)
+    arrive(slot(bq, xf, y), s_ax.at[xf])
+    send(slot(bq, xf, y), slot(bq, xf, y), s_ax.at[xf], dev(x + way, y, z, c))
+    spread_y(xf)
+    arrive(slot(bq, xb, y), s_ax.at[xb])
+    spread_y(xb)
+    for zz in (r4(z + way), r4(z + 2)):
+        arrive(stage.at[zz], s_z.at[zz])
+        arrive(dout.at[zz], s_d.at[zz])
+    for d in local:
+        d.wait()
+    for s in (1, 3, 2):
+        yt = r4(y + s)
+        send(stage.at[yt], slot(bp, x, y), s_by.at[y], dev(x, yt, z, c))
+    mine = pltpu.make_async_copy(stage.at[y], slot(bp, x, y), s_loc.at[3])
+    mine.start()
+
+    def spread_x(src, yy):
+        for s in (1, 3):
+            send(src, slot(bp, x, yy), s_bx.at[x, r4(yy)], dev(x + s, y, z, c))
+        send(src, slot(bp, x, yy), s_bs.at[x, r4(yy)], sib)
+
+    spread_x(stage.at[y], y)
+    x2 = r4(x + 2)
+    arrive(slot(bq, x2, y), s_ax.at[x2])
+    spread_y(x2)
+    for s in (1, 3, 2):
+        yy = r4(y + s)
+        arrive(slot(bp, x, yy), s_by.at[yy])
+        spread_x(slot(bp, x, yy), yy)
+    yf = r4(y - way)
+    for s, yy in ((0, y), (1, r4(y + 1)), (3, r4(y + 3)), (2, r4(y + 2))):
+        xx = r4((x, xf, xb, x2)[(0, 1, 3, 2).index(s)])
+        arrive(slot(bq, xx, yf), s_ay.at[xx, yf])
+        send(slot(bq, xx, yf), slot(bq, xx, yf), s_ay.at[xx, yf], dev(x, y + way, z, c))
+        send(slot(bq, xx, yf), slot(bq, xx, yf), s_as.at[xx, yf], sib)
+        arrive(slot(bp, xf, yy), s_bx.at[xf, yy])
+        send(slot(bp, xf, yy), slot(bp, xf, yy), s_bx.at[xf, yy], dev(x + way, y, z, c))
+        send(slot(bp, xf, yy), slot(bp, xf, yy), s_bs.at[xf, yy], sib)
+    yb, y2 = r4(y + way), r4(y + 2)
+    for ya, xa in ((yb, xb), (y2, x2)):
+        for s in range(4):
+            xx, yy = r4(x + s), r4(y + s)
+            arrive(slot(bq, xx, ya), s_ay.at[xx, ya])
+            send(slot(bq, xx, ya), slot(bq, xx, ya), s_as.at[xx, ya], sib)
+            arrive(slot(bp, xa, yy), s_bx.at[xa, yy])
+            send(slot(bp, xa, yy), slot(bp, xa, yy), s_bs.at[xa, yy], sib)
+    mine.wait()
+    for xx in range(4):
+        for yy in range(4):
+            arrive(slot(bq, xx, yy, o), s_as.at[xx, yy])
+            arrive(slot(bp, xx, yy, o), s_bs.at[xx, yy])
+    for d in sends:
+        d.wait_send()
+
+
+def gather(own, dens):
+    hbm = pl.BlockSpec(memory_space=pl.ANY)
+    n, dma = own.shape, pltpu.SemaphoreType.DMA
+    return pl.pallas_call(
+        gather_kernel,
+        out_shape=[
+            jax.ShapeDtypeStruct((32,) + n, own.dtype),
+            jax.ShapeDtypeStruct((32,) + n, own.dtype),
+            jax.ShapeDtypeStruct((4,) + dens.shape, dens.dtype),
+            jax.ShapeDtypeStruct((4,) + n, own.dtype),
+        ],
+        in_specs=[hbm] * 2,
+        out_specs=[hbm] * 4,
+        scratch_shapes=[dma((72,)), dma((4,)), dma((4,)), dma((4,)), dma((4, 4)), dma((4, 4)), dma((4,)), dma((4, 4)), dma((4, 4)), dma((4,))],
+        compiler_params=pltpu.CompilerParams(collective_id=0, has_side_effects=True),
+        name="gather",
+    )(own, dens)[:3]
+
+
+def reduce_kernel(part, out, got, cut, got2, send1, recv1, send2, recv2):
+    m, x, y, z, c = place()
+    g = lax.rem(m, 8)
+    near = [(y * 8 + lax.rem(g + d, 8), z) for d in range(1, 8)]
+    far = []
+    for d in range(1, 16):
+        h = lax.rem(y * 4 + z + d, 16)
+        far.append((h // 4, lax.rem(h, 4)))
+    greet(near + [((yy * 8 + g), zz) for yy, zz in far])
+    first = []
+    for d in range(1, 8):
+        gg = lax.rem(g + d, 8)
+        cp = pltpu.make_async_remote_copy(src_ref=part.at[:, gg], dst_ref=got.at[g], send_sem=send1.at[d], recv_sem=recv1.at[g], device_id=near[d - 1], device_id_type=MESH)
+        cp.start()
+        first.append(cp)
+    got[g] = part[:, g]
+    cut[...] = jnp.zeros_like(cut)
+    for d in range(1, 8):
+        gg = lax.rem(g + d, 8)
+        pltpu.make_async_remote_copy(src_ref=part.at[:, gg], dst_ref=got.at[gg], send_sem=send1.at[d], recv_sem=recv1.at[gg], device_id=near[0], device_id_type=MESH).wait_recv()
+    total = got[0]
+    for k in range(1, 8):
+        total = total + got[k]
+    for zz in range(4):
+        cut[:, zz, :, 0:48] = total[:, :, 48 * zz:48 * zz + 48]
+    second = []
+    for d, (yy, zz) in enumerate(far):
+        cp = pltpu.make_async_remote_copy(src_ref=cut.at[yy, zz], dst_ref=got2.at[y, z], send_sem=send2.at[d], recv_sem=recv2.at[y, z], device_id=(yy * 8 + g, zz), device_id_type=MESH)
+        cp.start()
+        second.append(cp)
+    got2[y, z] = cut[y, z]
+    for yy, zz in far:
+        pltpu.make_async_remote_copy(src_ref=cut.at[yy, zz], dst_ref=got2.at[yy, zz], send_sem=send2.at[0], recv_sem=recv2.at[yy, zz], device_id=(yy * 8 + g, zz), device_id_type=MESH).wait_recv()
+    result = got2[0, 0]
+    for k in range(1, 16):
+        result = result + got2[k // 4, k % 4]
+    out[...] = result
+    for cp in first + second:
+        cp.wait_send()
+
+
+def reduce(part):
+    vmem = pl.BlockSpec(memory_space=pltpu.VMEM)
+    dma = pltpu.SemaphoreType.DMA
+    return pl.pallas_call(
+        reduce_kernel,
+        out_shape=jax.ShapeDtypeStruct((8, 128), F32),
+        in_specs=[vmem],
+        out_specs=vmem,
+        scratch_shapes=[
+            pltpu.VMEM((8, 4, 8, 256), F32),
+            pltpu.VMEM((4, 4, 8, 128), F32),
+            pltpu.VMEM((4, 4, 8, 128), F32),
+            dma((8,)), dma((8,)), dma((16,)), dma((4, 4)),
+        ],
+        compiler_params=pltpu.CompilerParams(collective_id=1, has_side_effects=True),
+        name="reduce",
+    )(part)
+
+
 def body(block_list, block_values, atom_offsets, density, metric_inverse):
     m, r = lax.axis_index("map"), lax.axis_index("row")
-    row = m // 8
-    lists = lax.all_gather(block_list, ("map", "row"), axis=0).reshape(32, 4, 8, 3)
-    values = lax.all_gather(block_values.reshape(8, 36, 128), ("map", "row"), axis=0).reshape(32, 4, 8, 36, 128)
-    full = lax.all_gather(density, "row", axis=0, tiled=True)
-
-    def pick(x, at):
-        return lax.dynamic_index_in_dim(x, at, 1, keepdims=False).reshape((256,) + x.shape[3:])
     parity = m % 2
-    codeq, codep, starts, counts = tables(pick(lists, r), pick(lists, row), atom_offsets // 6, 3 * (m // 2) + parity, r * 12)
+    names = jnp.pad(block_list.astype(BF16), ((0, 0), (0, 125)))
+    own = jnp.concatenate([block_values.transpose(1, 2, 0, 3).reshape(36, 8, 128), names[None]], axis=0)
+    bq, bp, dens = gather(own, density)
+
+    def lists(b):
+        return b[:, 36, :, :3].reshape(256, 3).astype(I32)
+
+    def blocks(b):
+        return b[:, :36].transpose(0, 2, 1, 3).reshape(256, 36, 128)
+    codeq, codep, starts, counts = tables(lists(bq), lists(bp), atom_offsets // 6, 3 * (m // 2) + parity, r * 12)
     meta = jnp.concatenate([starts, counts, jnp.stack([parity, parity, parity, parity, parity]).astype(I32)])
-    part = contract(codeq, codep, meta, pick(values, r), pick(values, row), metric_inverse, full.T)
-    by_column = lax.psum_scatter(part, "row", scatter_dimension=1, tiled=True)
-    return lax.psum_scatter(by_column, "map", scatter_dimension=0, tiled=True)
+    part = contract(codeq, codep, meta, blocks(bq), blocks(bp), metric_inverse, dens.reshape(192, 192).T)
+    return reduce(part.reshape(4, 8, 8, 256))[:6, :48]
 
 
 def solution(mesh):

time: 331 us -> 143 us (0.43); the launches traced: 327 us -> 143 us
  blocking collectives: 196 us -> 0 us
  Pallas kernels: 67.4 us -> 128 us
  waiting for transfers between devices: 34.4 us -> 0 us
  between operations: 14.2 us -> 0.1 us
    unnamed x1 -> x0, blocking collectives: 123 us -> none
    all_gather x2 -> x0, blocking collectives: 72.6 us -> none  [the longest x1 60.9 us: body(): lax.all_gather(block_list, ('map', 'row'), axis=0).reshape(32, 4, 8, 3)]
    pallas_call x1 -> x3, Pallas kernels: 67.4 us -> 128 us  [the longest x1 68.2 us: contract(): pl.pallas_call(contract_kernel, out_shape=jax.ShapeDtypeStruct((256, 256)...]
    unnamed x3 -> x0, waiting for transfers between devices: 33.6 us -> none
    dynamic_slice x4 -> x0, local copies, waits for them, and re-layouts: 6.89 us -> none  [pick(): lax.dynamic_index_in_dim(x, at, 1, keepdims=False)]
    transpose x0 -> x3, local copies, waits for them, and re-layouts: none -> 6.19 us  [blocks(): return b[:, :36].transpose(0, 2, 1, 3).reshape(256, 36, 128)]
  transfers between devices with their start and end apart: 2 -> 0, of which waited for: 2 -> 0; matrix products, arithmetic and copies ran while one was open for 2% -> 0% of each run, Pallas kernels for 0% -> 0%
where the time goes in v2:
time: 143 us
  Pallas kernels  128 us (90%)
  local copies, waits for them, and re-layouts  10.6 us (7%)
  other arithmetic  4.43 us (3%)
    pallas_call x1, Pallas kernels, contract(): pl.pallas_call(contract_kernel, out_shape=jax.ShapeDtypeStruct((256, 256)...  68.2 us
    pallas_call x1, Pallas kernels, gather(): pl.pallas_call(gather_kernel, out_shape=[jax.ShapeDtypeStruct((32,) + n,...  33.4 us
    pallas_call x1, Pallas kernels, reduce(): pl.pallas_call(reduce_kernel, out_shape=jax.ShapeDtypeStruct((8, 128), F3...  26.3 us
    transpose x3, local copies, waits for them, and re-layouts, blocks(): return b[:, :36].transpose(0, 2, 1, 3).reshape(256, 36, 128)  6.19 us

profile of v2, /device:TPU:1, one launch (start us, length us, event | category | flops | bytes accessed | tf_op | source)
XLA Modules:
  0.0 143.0 jit_solution(5643107420072673006)
XLA Ops:
  0.0 0.0 copy-start.2
  0.0 0.7 convert_element_type.26
  0.7 0.1 copy.30
  0.8 1.5 %pad_maximum_fusion.own = bf16[37,8,128]{2,1,0:T(8,128)(2,1)} fusion(bf16[1,8,128]{2,1,0:T(8,128)(2,1)S(1)} %pad_bitcast_fusion, bf16[36,8,128]{2,1,0:T(8,128)(2,1)} %bitcast.44), kind=kLoop, calls=%fused_computation.8 | loop fusion | flops 37888 | bytes 151552 | tf_op jit(solution)/shard_map/concatenate | solution.py:365
  2.3 33.4 %gather.1 = (bf16[32,37,8,128]{3,2,1,0:T(8,128)(2,1)}, bf16[32,37,8,128]{3,2,1,0:T(8,128)(2,1)}, bf16[4,48,192]{2,1,0:T(8,128)(2,1)}, bf16[4,37,8,128]{3,2,1,0:T(8,128)(2,1)}) custom-call(bf16[37,8,128]{2,1,0:T(8,128)(2,1)} %pad_maximum_fusion.own, bf16[48,192]{1,0:T(8,128)(2,1)} %dens.1), custom_call_target="tpu_custom_call" | custom-call | tf_op jit(solution)/shard_map/gather/pallas_call | solution.py:285
  35.7 0.0 copy-start
  35.7 1.1 bitcast_convert_fusion
  36.8 0.1 slice_subtract_fusion
  36.9 0.1 copy.44
  37.0 0.1 copy.45
  37.1 0.1 subtract_shift-left_fusion
  37.2 0.1 copy.40
  37.3 0.1 copy.43
  37.4 0.0 copy-done.2
  37.4 0.1 select_reduce_fusion.4
  37.5 0.1 convert_reduce_fusion.1
  37.7 0.1 copy.46
  37.7 0.1 fusion
  37.9 0.6 concatenate.7.meta
  38.5 0.3 convert_reduce_fusion
  38.8 0.1 copy.47
  39.0 0.1 select_reduce_fusion
  39.1 0.6 fusion.2
  39.7 0.6 pad.9.codeq
  40.3 0.0 copy-done
  40.3 2.0 %slice_bitcast_fusion = (bf16[32,8,36,128]{3,1,2,0:T(8,128)(2,1)S(1)}, bf16[32,8,36,128]{3,1,2,0:T(8,128)(2,1)S(1)}) fusion(bf16[32,37,8,128]{3,2,1,0:T(8,128)(2,1)} %get-tuple-element.9, bf16[32,37,8,128]{3,2,1,0:T(8,128)(2,1)S(1)} %copy-done), kind=kLoop, calls=%fused_computation | loop fusion | bytes 9437184 | tf_op jit(solution)/shard_map/transpose | solution.py:372
  42.3 2.1 %copy.37 = bf16[32,8,36,128]{3,2,1,0:T(8,128)(2,1)} copy(bf16[32,8,36,128]{3,1,2,0:T(8,128)(2,1)S(1)} %get-tuple-element.24) | data formatting | bytes 4718592 | tf_op jit(solution)/shard_map/transpose | solution.py:372
  44.4 0.0 copy-start.1
  44.4 2.1 %copy.38 = bf16[32,8,36,128]{3,2,1,0:T(8,128)(2,1)} copy(bf16[32,8,36,128]{3,1,2,0:T(8,128)(2,1)S(1)} %get-tuple-element.23) | data formatting | bytes 4718592 | tf_op jit(solution)/shard_map/transpose | solution.py:372
  46.5 0.0 copy-done.1
  46.5 0.8 copy.39
  47.2 68.2 %contract.1 = f32[256,256]{1,0:T(8,128)} custom-call(s32[272]{0:T(512)} %pad.9.codeq, s32[256]{0:T(256)} %bitcast.51, s32[40]{0:T(128)} %concatenate.7.meta, bf16[256,36,128]{2,1,0:T(8,128)(2,1)} %bitcast.39, bf16[256,36,128]{2,1,0:T(8,128)(2,1)} %bitcast.40, bf16[192,1536]{1,0:T(8,128)(2,1)} %v.1, bf16[192,192]{1,0:T(8,128)(2,1)} %bitcast.42), custom_call_target="tpu_custom_call" | custom-call | tf_op jit(solution)/shard_map/contract/pallas_call | solution.py:112
  115.4 26.3 %reduce.1 = f32[8,128]{1,0:T(8,128)} custom-call(f32[4,8,8,256]{3,2,1,0:T(8,128)} %bitcast.41), custom_call_target="tpu_custom_call" | custom-call | tf_op jit(solution)/shard_map/reduce/pallas_call | solution.py:345
  141.8 1.3 copy.49
  (12 shorter events, 0.1 us)
Async XLA Ops:
  0.0 37.4 %copy-start.2 = (s32[32]{0:T(128)S(1)}, s32[32]{0:T(128)}, u32[]{:S(2)}) copy-start(s32[32]{0:T(128)} %param.7) | copy-start | bytes 388
  35.7 4.5 %copy-start = (bf16[32,37,8,128]{3,2,1,0:T(8,128)(2,1)S(1)}, bf16[32,37,8,128]{3,2,1,0:T(8,128)(2,1)}, u32[]{:S(2)}) copy-start(bf16[32,37,8,128]{3,2,1,0:T(8,128)(2,1)} %get-tuple-element.8) | copy-start | bytes 7274500
  44.4 2.1 %copy-start.1 = (bf16[4,48,192]{2,1,0:T(8,128)(2,1)S(1)}, bf16[4,48,192]{2,1,0:T(8,128)(2,1)}, u32[]{:S(2)}) copy-start(bf16[4,48,192]{2,1,0:T(8,128)(2,1)} %get-tuple-element.10) | copy-start | bytes 221188

commit v3 on v2

v3 whole, which is shorter than its diff:
```python
import jax
import jax.numpy as jnp
from jax import lax
from jax.experimental import pallas as pl
from jax.experimental.pallas import tpu as pltpu
from jax.sharding import PartitionSpec as P

HI = lax.Precision.HIGHEST
F32, BF16, I32 = jnp.float32, jnp.bfloat16, jnp.int32
NT = (((1,), (1,)), ((), ()))
MESH = pl.DeviceIdType.MESH
GROUP = 32
CHUNK = 16
XROWS = 44
XUN = 4
HN = 48
NB = 16


def iota(shape, axis):
    return lax.broadcasted_iota(I32, shape, axis)


def contract_kernel(codex, codep, meta, sig, bq, bp_hbm, vt, dexp_hbm, out, xbuf, hbuf, obuf, sbuf, ebuf, kbuf, bp, dexp, s_b, s_d):
    nf, nh = meta[33], meta[34]
    table = pltpu.make_async_copy(dexp_hbm, dexp, s_d.at[0])
    table.start()

    def fetch(t):
        return pltpu.make_async_copy(bp_hbm.at[codep[t] & 255], bp.at[t, 0:48], s_b.at[t])

    def f_step(t, carry):
        fetch(t).start()
        bp[t, 48:64] = jnp.zeros((16, 128), BF16)
        return carry

    lax.fori_loop(0, nf + nh, f_step, 0)
    low_half = iota((8, 128), 1) < 64

    def x_step(step, carry):
        for w in range(XUN):
            ch = XUN * step + w
            src = [codex[8 * ch + u] for u in range(8)]
            rows = jnp.concatenate([bq[s & 255] for s in src], axis=0)
            x = jnp.dot(rows, vt[meta[40 + ch]], preferred_element_type=F32)
            for u in range(8):
                tiles = [x[48 * u + 8 * j:48 * u + 8 * j + 8] for j in range(6)]
                whole = [t[:, :128] for t in tiles]
                half = [jnp.where(low_half, tiles[2 * j][:, 128:], tiles[2 * j + 1][:, 128:]) for j in range(3)]
                xbuf[src[u] >> 8] = jnp.stack(whole + half)
        return carry

    lax.fori_loop(0, (meta[35] + XUN - 1) // XUN, x_step, 0)
    kbuf[...] = jnp.zeros_like(kbuf)
    ebuf[...] = jnp.zeros_like(ebuf)
    sbuf[...] = (iota((256, 2048), 0) == sig[...]).astype(F32).astype(BF16)
    lane, sub = iota((8, 128), 1), iota((8, 128), 0)
    low_mask = (lane % 8 == sub) & (lane < 64)
    high_mask = (lane % 8 == sub) & (lane >= 64)
    row, col = iota((8, 256), 0), iota((8, 256), 1)
    even_device = (iota((64, 128), 0) * 0 + meta[36]) == 0
    left_lanes = iota((64, 128), 1) < 64
    none = jnp.zeros((64, 128), BF16)
    table.wait()

    def w_step(t, carry):
        fetch(t).wait()
        return carry

    lax.fori_loop(0, nf + nh, w_step, 0)

    def spread(ld, nu_a, lb, nu_b):
        a = dexp[ld, pl.ds(nu_a, 8, stride=0), :]
        b = dexp[lb, pl.ds(nu_b, 8, stride=0), :]
        return jnp.where(low_mask, a, jnp.where(high_mask, b, 0.0))

    def pair(h):
        n = h.shape[0] // 8
        both = jnp.concatenate([h[:, :128].reshape(n, 8, 128), h[:, 128:].reshape(n, 8, 128)], axis=1)
        return both.astype(BF16)

    def group(half, base, cnt):
        def h_step(t2, carry):
            at, ls = [], []
            for u in range(2):
                t = base + jnp.minimum(2 * t2 + u, cnt - 1)
                code = codep[t]
                at.append(t)
                ls.append((code >> 8) & 31)
                ebuf[pl.ds(pl.multiple_of(16 * t2 + 8 * u, 8), 8), :] = (col == 8 * (code >> 13) + row).astype(F32)
            b0, b1 = bp[at[0]], bp[at[1]]
            if not half:
                rhs = jnp.concatenate([jnp.concatenate([b0, none], axis=1), jnp.concatenate([none, b1], axis=1)], axis=0)
                for c in range(0, 192, HN):
                    w = jnp.concatenate([spread(ls[0], nu, ls[1], nu) for nu in range(c, c + HN)], axis=0).astype(BF16)
                    hbuf[c:c + HN, t2] = pair(jnp.dot(w, rhs, preferred_element_type=F32))
            else:
                quads = []
                for b in (b0, b1):
                    wide = b.astype(F32)
                    turned = pltpu.roll(wide, 64, 1)
                    first = jnp.where(even_device, wide, turned)
                    second = jnp.where(even_device, turned, wide)
                    quads.append((jnp.where(left_lanes, first, 0.0).astype(BF16), jnp.where(left_lanes, 0.0, second).astype(BF16)))
                (e0, o0), (e1, o1) = quads
                rhs = jnp.concatenate([jnp.concatenate([p, q], axis=1) for p, q in ((e0, none), (o0, none), (none, e1), (none, o1))], axis=0)
                for c in range(0, 96, HN):
                    w = jnp.concatenate([
                        jnp.concatenate([spread(l, 2 * r, l, 2 * r + 1) for r in range(c, c + HN)], axis=0).astype(BF16)
                        for l in ls], axis=1)
                    hbuf[c:c + HN, t2] = pair(jnp.dot(w, rhs, preferred_element_type=F32))
            return carry

        lax.fori_loop(0, (cnt + 1) // 2, h_step, 0)
        depth, first = (3, 6) if half else (6, 0)

        def chunk(n, k0):
            xs = jnp.concatenate([xbuf[pl.ds(k0, CHUNK), first + j].reshape(CHUNK * 8, 128).astype(BF16) for j in range(depth)], axis=1)
            hs = jnp.concatenate([hbuf[n * depth + j].reshape(GROUP * 8, 128) for j in range(depth)], axis=1)
            o = lax.dot_general(xs, hs, NT, preferred_element_type=F32)
            obuf[pl.ds(pl.multiple_of(8 * k0, 8), CHUNK * 8), :] = o

        def n_step(i, carry):
            ends = [meta[NB * i + u] for u in range(NB + 1)]
            for u in range(NB):
                chunk(NB * i + u, ends[u])
            longest = ends[1] - ends[0]
            for u in range(1, NB):
                longest = jnp.maximum(longest, ends[u + 1] - ends[u])

            @pl.when(longest > CHUNK)
            def _():
                def again(n, carry):
                    s0, s1 = meta[n], meta[n + 1]

                    def c_step(c, carry):
                        chunk(n, s0 + CHUNK * c)
                        return carry

                    return lax.fori_loop(0, (s1 - s0 + CHUNK - 1) // CHUNK, c_step, carry)

                lax.fori_loop(NB * i, NB * i + NB, again, 0)
            return carry

        lax.fori_loop(0, 32 // NB, n_step, 0)
        r = jnp.zeros((256, 256), F32)
        for k in range(8):
            o = obuf[256 * k:256 * k + 256, :]
            high = o.astype(BF16)
            low = (o - high.astype(F32)).astype(BF16)
            s = sbuf[:, 256 * k:256 * k + 256]
            r += jnp.dot(s, high, preferred_element_type=F32) + jnp.dot(s, low, preferred_element_type=F32)
        r = jnp.where(iota((256, 256), 1) < 8 * cnt, r, 0.0)
        kbuf[...] += jnp.dot(r, ebuf[...], preferred_element_type=F32, precision=HI)

    for half, base, total in ((False, 0, nf), (True, nf, nh)):
        def g_step(g, carry, half=half, base=base, total=total):
            group(half, base + GROUP * g, jnp.minimum(total - GROUP * g, GROUP))
            return carry

        lax.fori_loop(0, (total + GROUP - 1) // GROUP, g_step, 0)
    out[...] = kbuf[...].T


def contract(codex, codep, meta, sig, bq, bp, vt, dexp):
    smem = pl.BlockSpec(memory_space=pltpu.SMEM)
    vmem = pl.BlockSpec(memory_space=pltpu.VMEM)
    hbm = pl.BlockSpec(memory_space=pl.ANY)
    return pl.pallas_call(
        contract_kernel,
        out_shape=jax.ShapeDtypeStruct((256, 256), F32),
        in_specs=[smem] * 3 + [vmem, vmem, hbm, vmem, hbm],
        out_specs=vmem,
        scratch_shapes=[
            pltpu.VMEM((256 + CHUNK, 9, 8, 128), F32),
            pltpu.VMEM((192, GROUP // 2, 16, 128), BF16),
            pltpu.VMEM(((256 + CHUNK) * 8, 256), F32),
            pltpu.VMEM((256, 2048), BF16),
            pltpu.VMEM((256, 256), F32),
            pltpu.VMEM((256, 256), F32),
            pltpu.VMEM((256, 64, 128), BF16),
            pltpu.VMEM((32, 192, 128), F32),
            pltpu.SemaphoreType.DMA((256,)),
            pltpu.SemaphoreType.DMA((1,)),
        ],
        compiler_params=pltpu.CompilerParams(vmem_limit_bytes=60 << 20),
        name="contract",
    )(codex, codep, meta, sig, bq, bp, vt, dexp)


def tables(listq, listp, slots, whole_block, half_block, row_start, parity):
    at = jnp.arange(256, dtype=I32)

    def slot(x):
        return jnp.sum(jnp.where(x[:, None] == jnp.arange(32, dtype=I32), slots, 0), axis=1)

    def count(keys, upto):
        return jnp.sum((keys[None, :] < upto[:, None]).astype(I32), axis=1)

    def rank(key):
        before = (key[None, :] < key[:, None]) | ((key[None, :] == key[:, None]) & (at[None, :] < at[:, None]))
        return jnp.sum(before.astype(I32), axis=1)

    def place(where, n, code, rest):
        hit = where[None, :] == jnp.arange(n, dtype=I32)[:, None]
        return rest + jnp.sum(jnp.where(hit, code[None, :] - rest, 0), axis=1)

    q = listq[:, 2] - row_start
    by_n = rank(slot(listq[:, 1]))
    starts = count(slot(listq[:, 1]), jnp.arange(33, dtype=I32))
    sig = 6 * place(by_n, 256, slot(listq[:, 0]), 0)[:, None] + jnp.arange(8, dtype=I32)
    sig = jnp.where(jnp.arange(8) < 6, sig, -1).reshape(1, 2048)
    ends = jnp.cumsum((count(q, jnp.arange(1, 13, dtype=I32)) - count(q, jnp.arange(12, dtype=I32)) + 7) // 8)
    lead = 8 * jnp.sum(jnp.where(q[:, None] > jnp.arange(12, dtype=I32), (ends - jnp.concatenate([ends[:1] * 0, ends[:-1]]))[None, :], 0), axis=1)
    within = rank(q) - jnp.sum((q[None, :] < q[:, None]).astype(I32), axis=1)
    codex = place(lead + within, 8 * XROWS, at + (by_n << 8), 256 << 8)
    chunk_q = jnp.minimum(jnp.sum((ends[None, :] <= jnp.arange(XROWS, dtype=I32)[:, None]).astype(I32), axis=1), 11)
    p = listp[:, 2]
    keyp = jnp.where(p == whole_block, 0, jnp.where(p == half_block, 1, 2))
    codep = place(rank(keyp), 256, at + (slot(listp[:, 1]) << 8) + (slot(listp[:, 0]) << 13), 0)
    counts = jnp.stack([jnp.sum((keyp == 0).astype(I32)), jnp.sum((keyp == 1).astype(I32))])
    meta = jnp.concatenate([starts, counts, ends[11:], jnp.stack([parity] * 4).astype(I32), chunk_q])
    return codex, codep, meta, sig


def place():
    m, z = lax.axis_index("map"), lax.axis_index("row")
    return m, (m // 2) % 4, m // 8, z, m % 2


def at_map(x, y, c):
    return (y * 4 + x) * 2 + c


def greet(devices, between=None):
    barrier = pltpu.get_barrier_semaphore()
    for d in devices:
        pl.semaphore_signal(barrier, inc=1, device_id=d, device_id_type=MESH)
    if between is not None:
        between()
    pl.semaphore_wait(barrier, len(devices))


ROWS = 304


def gather_kernel(own, names, dens, v, wide_q, wide_p, names_q, names_p, vt_out, dexp_out, bq, bp, stage, dall, held, vbuf, vt, dexp, wq, wp, spread, s_send, s_z, s_d, s_ax, s_ay, s_as, s_by, s_bx, s_bs, s_loc, s_wq, s_wp):
    m, x, y, z, c = place()
    way = 1 - 2 * c
    o = 1 - c

    def dev(xx, yy, zz, cc):
        return (at_map(lax.rem(xx + 4, 4), lax.rem(yy + 4, 4), cc), lax.rem(zz + 4, 4))

    def r4(v):
        return lax.rem(v + 8, 4)

    def index(xx, yy, cc=None):
        return at_map(r4(xx), r4(yy), c if cc is None else cc)

    sib = dev(x, y, z, o)
    mine_at = index(x, y)
    first = [
        pltpu.make_async_copy(own, bq.at[mine_at, 0:288], s_loc.at[0]),
        pltpu.make_async_copy(names, bq.at[mine_at, 288:304], s_loc.at[1]),
        pltpu.make_async_copy(dens, dall.at[z], s_loc.at[2]),
        pltpu.make_async_copy(v, held, s_loc.at[3]),
    ]
    for d in first:
        d.start()

    def between():
        r, k = iota((384, 288), 0), iota((384, 288), 1)
        block, j, i = r // 48, (r % 48) // 8, r % 8
        spread[...] = ((k % 8 == block) & (k // 8 == i * 6 + j) & (i < 6)).astype(F32).astype(BF16)
        for d in first[:3]:
            d.wait()

    greet([dev(x + 1, y, z, c), dev(x + 3, y, z, c), dev(x, y + 1, z, c), dev(x, y + 3, z, c), dev(x, y + 2, z, c), dev(x, y, z + 1, c), dev(x, y, z + 3, c), sib], between)
    sends = []

    def send(src, dst, recv, device):
        n = len(sends)
        d = pltpu.make_async_remote_copy(src_ref=src, dst_ref=dst, send_sem=s_send.at[n], recv_sem=recv, device_id=device, device_id_type=MESH)
        d.start()
        sends.append(d)

    def arrive(dst, recv):
        pltpu.make_async_remote_copy(src_ref=dst, dst_ref=dst, send_sem=s_send.at[0], recv_sem=recv, device_id=sib, device_id_type=MESH).wait_recv()

    def slot(ref, xx, yy, cc=None):
        return ref.at[index(xx, yy, cc)]

    written = []

    def widen(ref, at, buf, out, sem):
        got = ref[at]
        buf[at] = jnp.dot(spread[...], got[0:288], preferred_element_type=F32).astype(BF16)
        d = pltpu.make_async_copy(buf.at[at], out.at[at], sem.at[at])
        d.start()
        written.append(d)

    def wide_of_q(xx, yy, cc=None):
        widen(bq, index(xx, yy, cc), wq, wide_q, s_wq)

    def wide_of_p(xx, yy, cc=None):
        widen(bp, index(xx, yy, cc), wp, wide_p, s_wp)

    own_piece = slot(bq, x, y)
    for s in (1, 3):
        send(own_piece, stage.at[z], s_z.at[z], dev(x, y, z + s, c))
        send(dall.at[z], dall.at[z], s_d.at[z], dev(x, y, z + s, c))
    for s in (1, 3):
        send(own_piece, own_piece, s_ax.at[x], dev(x + s, y, z, c))
    for s in (1, 3):
        send(own_piece, own_piece, s_ay.at[x, y], dev(x, y + s, z, c))
    send(own_piece, own_piece, s_as.at[x, y], sib)
    keep = pltpu.make_async_copy(own_piece, stage.at[z], s_loc.at[0])
    keep.start()
    wide_of_q(x, y)
    zf = r4(z - way)
    arrive(stage.at[zf], s_z.at[zf])
    send(stage.at[zf], stage.at[zf], s_z.at[zf], dev(x, y, z + way, c))
    arrive(dall.at[zf], s_d.at[zf])
    send(dall.at[zf], dall.at[zf], s_d.at[zf], dev(x, y, z + way, c))

    def spread_y(xx):
        for s in (1, 3):
            send(slot(bq, xx, y), slot(bq, xx, y), s_ay.at[r4(xx), y], dev(x, y + s, z, c))
        send(slot(bq, xx, y), slot(bq, xx, y), s_as.at[r4(xx), y], sib)

    xf, xb = r4(x - way), r4(x + way)
    arrive(slot(bq, xf, y), s_ax.at[xf])
    send(slot(bq, xf, y), slot(bq, xf, y), s_ax.at[xf], dev(x + way, y, z, c))
    spread_y(xf)
    arrive(slot(bq, xb, y), s_ax.at[xb])
    spread_y(xb)
    for zz in (r4(z + way), r4(z + 2)):
        arrive(stage.at[zz], s_z.at[zz])
        arrive(dall.at[zz], s_d.at[zz])
    keep.wait()
    for s in (1, 3, 2):
        yt = r4(y + s)
        send(stage.at[yt], slot(bp, x, y), s_by.at[y], dev(x, yt, z, c))
    mine = pltpu.make_async_copy(stage.at[y], slot(bp, x, y), s_loc.at[1])
    mine.start()

    def spread_x(src, yy):
        for s in (1, 3):
            send(src, slot(bp, x, yy), s_bx.at[x, r4(yy)], dev(x + s, y, z, c))
        send(src, slot(bp, x, yy), s_bs.at[x, r4(yy)], sib)

    spread_x(stage.at[y], y)
    x2 = r4(x + 2)
    arrive(slot(bq, x2, y), s_ax.at[x2])
    spread_y(x2)
    first[3].wait()
    parity = lax.rem(m, 2)
    vbuf[0:128] = held[pl.ds(pl.multiple_of(64 * parity, 64), 128), :]
    half = held[pl.ds(pl.multiple_of(128 * (1 - parity), 64), 64), :]
    vbuf[128:192] = half
    vbuf[192:256] = half
    same = (iota((128, 128), 0) == iota((128, 128), 1)).astype(F32).astype(BF16)
    for q in range(12):
        vt[q] = lax.dot_general(same, vbuf[:, 128 * q:128 * q + 128], NT, preferred_element_type=F32).astype(BF16)
    vt_copy = pltpu.make_async_copy(vt, vt_out, s_loc.at[2])
    vt_copy.start()
    for s in (1, 3, 2):
        yy = r4(y + s)
        arrive(slot(bp, x, yy), s_by.at[yy])
        spread_x(slot(bp, x, yy), yy)
    mine.wait()
    same = (iota((192, 192), 0) == iota((192, 192), 1)).astype(F32).astype(BF16)
    full = jnp.concatenate([dall[k] for k in range(4)], axis=0)
    turned = lax.dot_general(same, full, NT, preferred_element_type=F32).astype(BF16)
    lam, lane = iota((192, 128), 0), iota((192, 128), 1)
    part = (lane % 64) // 8
    for l in range(32):
        sel = ((lam == 6 * l + part) & (part < 6)).astype(F32).astype(BF16)
        dexp[l] = jnp.dot(turned, sel, preferred_element_type=F32)
    dexp_copy = pltpu.make_async_copy(dexp, dexp_out, s_loc.at[0])
    dexp_copy.start()
    for xx in (xf, xb, x2):
        wide_of_q(xx, y)
    yf = r4(y - way)
    for xx, yy in ((x, y), (xf, r4(y + 1)), (xb, r4(y + 3)), (x2, r4(y + 2))):
        arrive(slot(bq, xx, yf), s_ay.at[xx, yf])
        send(slot(bq, xx, yf), slot(bq, xx, yf), s_ay.at[xx, yf], dev(x, y + way, z, c))
        send(slot(bq, xx, yf), slot(bq, xx, yf), s_as.at[xx, yf], sib)
        arrive(slot(bp, xf, yy), s_bx.at[xf, yy])
        send(slot(bp, xf, yy), slot(bp, xf, yy), s_bx.at[xf, yy], dev(x + way, y, z, c))
        send(slot(bp, xf, yy), slot(bp, xf, yy), s_bs.at[xf, yy], sib)
        wide_of_p(x, yy)
        wide_of_q(xx, yf)
        wide_of_p(xf, yy)
    yb, y2 = r4(y + way), r4(y + 2)
    for ya, xa in ((yb, xb), (y2, x2)):
        for s in range(4):
            xx, yy = r4(x + s), r4(y + s)
            arrive(slot(bq, xx, ya), s_ay.at[xx, ya])
            send(slot(bq, xx, ya), slot(bq, xx, ya), s_as.at[xx, ya], sib)
            arrive(slot(bp, xa, yy), s_bx.at[xa, yy])
            send(slot(bp, xa, yy), slot(bp, xa, yy), s_bs.at[xa, yy], sib)
            wide_of_q(xx, ya)
            wide_of_p(xa, yy)
    for xx, xp in ((x, x), (xf, xf), (xb, xb), (x2, x2)):
        for yy in (y, yf, yb, y2):
            arrive(slot(bq, xx, yy, o), s_as.at[xx, yy])
            wide_of_q(xx, yy, o)
            arrive(slot(bp, xx, yy, o), s_bs.at[xx, yy])
            wide_of_p(xx, yy, o)
    last = [
        pltpu.make_async_copy(bq.at[:, 288:304], names_q, s_loc.at[1]),
        pltpu.make_async_copy(bp.at[:, 288:304], names_p, s_loc.at[3]),
    ]
    for d in last:
        d.start()
    for d in written + last + [vt_copy, dexp_copy]:
        d.wait()
    for d in sends:
        d.wait_send()


def gather(own, names, dens, v):
    hbm = pl.BlockSpec(memory_space=pl.ANY)
    dma = pltpu.SemaphoreType.DMA
    return pl.pallas_call(
        gather_kernel,
        out_shape=[
            jax.ShapeDtypeStruct((32, 384, 128), BF16),
            jax.ShapeDtypeStruct((32, 384, 128), BF16),
            jax.ShapeDtypeStruct((32, 16, 128), BF16),
            jax.ShapeDtypeStruct((32, 16, 128), BF16),
            jax.ShapeDtypeStruct((12, 128, 256), BF16),
            jax.ShapeDtypeStruct((32, 192, 128), F32),
        ],
        in_specs=[hbm] * 4,
        out_specs=[hbm] * 6,
        scratch_shapes=[
            pltpu.VMEM((32, ROWS, 128), BF16),
            pltpu.VMEM((32, ROWS, 128), BF16),
            pltpu.VMEM((4, ROWS, 128), BF16),
            pltpu.VMEM((4, 48, 192), BF16),
            pltpu.VMEM((192, 1536), BF16),
            pltpu.VMEM((256, 1536), BF16),
            pltpu.VMEM((12, 128, 256), BF16),
            pltpu.VMEM((32, 192, 128), F32),
            pltpu.VMEM((32, 384, 128), BF16),
            pltpu.VMEM((32, 384, 128), BF16),
            pltpu.VMEM((384, 288), BF16),
            dma((72,)), dma((4,)), dma((4,)), dma((4,)), dma((4, 4)), dma((4, 4)), dma((4,)), dma((4, 4)), dma((4, 4)), dma((4,)), dma((32,)), dma((32,)),
        ],
        compiler_params=pltpu.CompilerParams(collective_id=0, has_side_effects=True, vmem_limit_bytes=48 << 20),
        name="gather",
    )(own, names, dens, v)


def reduce_kernel(part, out, got, cut, got2, send1, recv1, send2, recv2):
    m, x, y, z, c = place()
    g = lax.rem(m, 8)
    near = [(y * 8 + lax.rem(g + d, 8), z) for d in range(1, 8)]
    far = []
    for d in range(1, 16):
        h = lax.rem(y * 4 + z + d, 16)
        far.append((h // 4, lax.rem(h, 4)))
    greet(near + [((yy * 8 + g), zz) for yy, zz in far])
    first = []
    for d in range(1, 8):
        gg = lax.rem(g + d, 8)
        cp = pltpu.make_async_remote_copy(src_ref=part.at[:, gg], dst_ref=got.at[g], send_sem=send1.at[d], recv_sem=recv1.at[g], device_id=near[d - 1], device_id_type=MESH)
        cp.start()
        first.append(cp)
    got[g] = part[:, g]
    cut[...] = jnp.zeros_like(cut)
    for d in range(1, 8):
        gg = lax.rem(g + d, 8)
        pltpu.make_async_remote_copy(src_ref=part.at[:, gg], dst_ref=got.at[gg], send_sem=send1.at[d], recv_sem=recv1.at[gg], device_id=near[0], device_id_type=MESH).wait_recv()
    total = got[0]
    for k in range(1, 8):
        total = total + got[k]
    for zz in range(4):
        cut[:, zz, :, 0:48] = total[:, :, 48 * zz:48 * zz + 48]
    second = []
    for d, (yy, zz) in enumerate(far):
        cp = pltpu.make_async_remote_copy(src_ref=cut.at[yy, zz], dst_ref=got2.at[y, z], send_sem=send2.at[d], recv_sem=recv2.at[y, z], device_id=(yy * 8 + g, zz), device_id_type=MESH)
        cp.start()
        second.append(cp)
    got2[y, z] = cut[y, z]
    for yy, zz in far:
        pltpu.make_async_remote_copy(src_ref=cut.at[yy, zz], dst_ref=got2.at[yy, zz], send_sem=send2.at[0], recv_sem=recv2.at[yy, zz], device_id=(yy * 8 + g, zz), device_id_type=MESH).wait_recv()
    result = got2[0, 0]
    for k in range(1, 16):
        result = result + got2[k // 4, k % 4]
    out[...] = result
    for cp in first + second:
        cp.wait_send()


def reduce(part):
    vmem = pl.BlockSpec(memory_space=pltpu.VMEM)
    dma = pltpu.SemaphoreType.DMA
    return pl.pallas_call(
        reduce_kernel,
        out_shape=jax.ShapeDtypeStruct((8, 128), F32),
        in_specs=[vmem],
        out_specs=vmem,
        scratch_shapes=[
            pltpu.VMEM((8, 4, 8, 256), F32),
            pltpu.VMEM((4, 4, 8, 128), F32),
            pltpu.VMEM((4, 4, 8, 128), F32),
            dma((8,)), dma((8,)), dma((16,)), dma((4, 4)),
        ],
        compiler_params=pltpu.CompilerParams(collective_id=1, has_side_effects=True),
        name="reduce",
    )(part)


def body(block_list, block_values, atom_offsets, density, metric_inverse):
    m, r = lax.axis_index("map"), lax.axis_index("row")
    parity, chip = m % 2, m // 2
    names = jnp.pad(block_list.astype(BF16), ((0, 8), (0, 125)))
    own = block_values.transpose(1, 2, 0, 3).reshape(288, 128)
    bq, bp, names_q, names_p, vt, dexp = gather(own, names, density, metric_inverse)

    def lists(b):
        return b[:, :8, :3].reshape(256, 3).astype(I32)
    codex, codep, meta, sig = tables(lists(names_q), lists(names_p), atom_offsets // 6, 3 * chip + 2 * parity, 3 * chip + 1, r * 12, parity)
    part = contract(codex, codep, meta, sig, bq.reshape(256, 48, 128), bp.reshape(256, 48, 128), vt, dexp)
    return reduce(part.reshape(4, 8, 8, 256))[:6, :48]


def solution(mesh):
    placed = (
        P(("map", "row"), None),
        P(("map", "row"), None, None, None),
        P(),
        P("row", None),
        P("map", "row"),
    )
    return jax.shard_map(
        body, mesh=mesh, in_specs=placed, out_specs=P("map", "row"), check_vma=False
    )
```

time: 143 us -> 108 us (0.76)
  Pallas kernels: 128 us -> 91.4 us
    pallas_call x1, Pallas kernels: 68.2 us -> 27.2 us  [contract(): pl.pallas_call(contract_kernel, out_shape=jax.ShapeDtypeStruct((256, 256)...]
    pallas_call x1, Pallas kernels: 33.4 us -> 41.3 us  [gather(): pl.pallas_call(gather_kernel, out_shape=[jax.ShapeDtypeStruct((32, 384, 1...]
    transpose x3 -> x0, local copies, waits for them, and re-layouts: 6.19 us -> none  [blocks(): return b[:, :36].transpose(0, 2, 1, 3).reshape(256, 36, 128)]
    unnamed x13 -> x17, local copies, waits for them, and re-layouts: 1.77 us -> 7.01 us
    pallas_call x1, Pallas kernels: 26.3 us -> 22.9 us  [reduce(): pl.pallas_call(reduce_kernel, out_shape=jax.ShapeDtypeStruct((8, 128), F3...]
    reduce_sum x4 -> x11, other arithmetic: 0.68 us -> 2.7 us  [the longest x3 0.91 us: place(): return rest + jnp.sum(jnp.where(hit, code[None, :] - rest, 0), axis=1)]
    concatenate x1 -> x2, local copies, waits for them, and re-layouts: 0.62 us -> 2.57 us  [the longest x1 2.56 us: tables(): jnp.concatenate([starts, counts, ends[11:], jnp.stack([parity] * 4).astyp...]
    concatenate x1 -> x0, other arithmetic: 1.52 us -> none  [body(): jnp.concatenate([block_values.transpose(1, 2, 0, 3).reshape(36, 8, 128),...]
where the time goes in v3:
time: 108 us
  Pallas kernels  91.4 us (85%)
  local copies, waits for them, and re-layouts  11.1 us (10%)
  other arithmetic  5.33 us (5%)
    pallas_call x1, Pallas kernels, gather(): pl.pallas_call(gather_kernel, out_shape=[jax.ShapeDtypeStruct((32, 384, 1...  41.3 us
    pallas_call x1, Pallas kernels, contract(): pl.pallas_call(contract_kernel, out_shape=jax.ShapeDtypeStruct((256, 256)...  27.2 us
    pallas_call x1, Pallas kernels, reduce(): pl.pallas_call(reduce_kernel, out_shape=jax.ShapeDtypeStruct((8, 128), F3...  22.9 us
    unnamed x17, local copies, waits for them, and re-layouts  7.01 us
    concatenate x1, local copies, waits for them, and re-layouts, tables(): jnp.concatenate([starts, counts, ends[11:], jnp.stack([parity] * 4).astyp...  2.56 us

profile of v3, /device:TPU:1, one launch (start us, length us, event | category | flops | bytes accessed | tf_op | source)
XLA Modules:
  0.0 107.9 jit_solution(12863533773551819649)
XLA Ops:
  0.0 0.7 and_select_fusion
  0.7 0.7 convert_element_type.47
  1.4 0.1 copy.21
  1.5 0.0 copy-start.2
  1.5 1.1 copy-done.2
  2.5 0.0 copy-start.3
  2.5 0.9 copy-done.3
  3.4 0.0 copy-start.4
  3.4 0.7 copy-done.4
  4.2 41.3 %gather.1 = (bf16[32,384,128]{2,1,0:T(8,128)(2,1)S(1)}, bf16[32,384,128]{2,1,0:T(8,128)(2,1)}, bf16[32,16,128]{2,1,0:T(8,128)(2,1)S(1)}, bf16[32,16,128]{2,1,0:T...) custom-call(bf16[288,128]{1,0:T(8,128)(2,1)S(1)} %bitcast.36, ...), custom_call_target="tpu_custom_call" | custom-call | tf_op jit(solution)/shard_map/gather/pallas_call | solution.py:427
  45.5 0.0 copy-start
  45.5 1.7 %copy-done = bf16[32,384,128]{2,1,0:T(8,128)(2,1)} copy-done((bf16[32,384,128]{2,1,0:T(8,128)(2,1)}, bf16[32,384,128]{2,1,0:T(8,128)(2,1)S(1)}, u32[]{:S(2)}) %copy-start) | copy-done | bytes 3145752
  47.2 0.0 copy-start.1
  47.2 0.9 copy-done.1
  48.1 0.1 fusion.8
  48.2 0.1 copy.30
  48.3 0.2 convert_reduce_fusion
  48.5 0.7 fusion.7
  49.2 0.1 copy.31
  49.3 0.1 copy.32
  49.4 0.1 slice_subtract_fusion
  49.5 0.1 copy.34
  49.6 0.2 convert_reduce_fusion.4
  49.8 0.2 reduce-window.4
  50.0 0.6 slice.46
  50.6 0.1 convert_reduce_fusion.6
  50.7 0.1 add_subtract_fusion
  50.8 0.1 select_reduce_fusion.7
  50.9 0.1 copy.29
  51.0 0.1 copy.33
  51.0 0.1 select_reduce_fusion.3
  51.2 0.1 convert_reduce_fusion.3
  51.3 2.6 %concatenate.14.meta = s32[84]{0:T(128)} concatenate(s32[33]{0:T(128)S(1)} %convert_reduce_fusion.3, s32[1]{0:T(128)} %bitcast.12, s32[1]{0:T(128)} %bitcast.13, s32[1]{0:T(128)} %bitcast.14, s32[1]{0:T(128)} %bitcast.15, s32[1]{0:T(128)} %bitcast.15, s32[1]{0:T(128)} %bitcast.15, s32[1]{0:T(128)} %bitcast.15, s32[44]{0:T(128)S(1)} %broadcast_minimum_fusion), dimensions={0} | concatenate | bytes 672 | tf_op jit(solution)/shard_map/concatenate | solution.py:222
  53.8 0.2 convert_reduce_fusion.1
  54.0 0.1 select_reduce_fusion.1
  54.2 0.6 select_reduce_fusion.2.codep
  54.8 0.2 fusion
  55.0 0.1 select_reduce_fusion
  55.2 0.6 broadcast_add_fusion.codex
  55.8 0.1 add_select_fusion
  55.9 0.7 select_n.109.sig
  56.6 27.2 %contract.1 = f32[256,256]{1,0:T(8,128)} custom-call(s32[352]{0:T(512)} %broadcast_add_fusion.codex, s32[256]{0:T(256)} %select_reduce_fusion.2.codep, s32[84]{0:T(128)} %concatenate.14.meta, s32[1,2048]{1,0:T(1,128)} %select_n.109.sig, bf16[256,48,128]{2,1,0:T(8,128)(2,1)} %bitcast.35, bf16[256,48,128]{2,1,0:T(8,128)(2,1)} %bitcast.37, ...), custom_call_target="tpu_custom_call" | custom-call | tf_op jit(solution)/shard_map/contract/pallas_call | solution.py:169
  83.8 22.9 %reduce.1 = f32[8,128]{1,0:T(8,128)} custom-call(f32[4,8,8,256]{3,2,1,0:T(8,128)} %bitcast.38), custom_call_target="tpu_custom_call" | custom-call | tf_op jit(solution)/shard_map/reduce/pallas_call | solution.py:502
  106.7 1.3 %copy.36 = f32[6,48]{1,0:T(8,128)} copy(f32[6,48]{1,0:T(8,128)} %bitcast.42) | data formatting | bytes 2304
  (12 shorter events, 0.1 us)
Async XLA Ops:
  1.5 1.1 copy-start.2
  2.5 0.9 copy-start.3
  3.4 0.7 copy-start.4
  45.5 1.7 %copy-start = (bf16[32,384,128]{2,1,0:T(8,128)(2,1)}, bf16[32,384,128]{2,1,0:T(8,128)(2,1)S(1)}, u32[]{:S(2)}) copy-start(bf16[32,384,128]{2,1,0:T(8,128)(2,1)S(1)} %get-tuple-element.13) | copy-start | bytes 9437188
  47.2 0.9 copy-start.1

commit v4 on v3

--- a/solution.py
+++ b/solution.py
@@ -223,6 +223,10 @@
     return codex, codep, meta, sig
 
 
+ROWS = 304
+XDIRECT = True
+
+
 def place():
     m, z = lax.axis_index("map"), lax.axis_index("row")
     return m, (m // 2) % 4, m // 8, z, m % 2
@@ -241,28 +245,22 @@
     pl.semaphore_wait(barrier, len(devices))
 
 
-ROWS = 304
-
-
-def gather_kernel(own, names, dens, v, wide_q, wide_p, names_q, names_p, vt_out, dexp_out, bq, bp, stage, dall, held, vbuf, vt, dexp, wq, wp, spread, s_send, s_z, s_d, s_ax, s_ay, s_as, s_by, s_bx, s_bs, s_loc, s_wq, s_wp):
+def gather_kernel(own, names, dens, v, wide_q, wide_p, vt_out, dexp_out, bq, bp, stage, dall, held, vbuf, vt, dexp, wq, wp, spread, s_send, s_z, s_d, s_ax, s_ay, s_as, s_by, s_bx, s_bs, s_loc, s_wq, s_wp):
     m, x, y, z, c = place()
     way = 1 - 2 * c
     o = 1 - c
 
-    def dev(xx, yy, zz, cc):
-        return (at_map(lax.rem(xx + 4, 4), lax.rem(yy + 4, 4), cc), lax.rem(zz + 4, 4))
-
     def r4(v):
         return lax.rem(v + 8, 4)
 
-    def index(xx, yy, cc=None):
-        return at_map(r4(xx), r4(yy), c if cc is None else cc)
+    def dev(xx, yy, zz, cc):
+        return (at_map(r4(xx), r4(yy), cc), r4(zz))
 
     sib = dev(x, y, z, o)
-    mine_at = index(x, y)
+    own_piece = bq.at[y, x]
     first = [
-        pltpu.make_async_copy(own, bq.at[mine_at, 0:288], s_loc.at[0]),
-        pltpu.make_async_copy(names, bq.at[mine_at, 288:304], s_loc.at[1]),
+        pltpu.make_async_copy(own, bq.at[y, x, 0:288], s_loc.at[0]),
+        pltpu.make_async_copy(names, bq.at[y, x, 288:304], s_loc.at[1]),
         pltpu.make_async_copy(dens, dall.at[z], s_loc.at[2]),
         pltpu.make_async_copy(v, held, s_loc.at[3]),
     ]
@@ -270,13 +268,14 @@
         d.start()
 
     def between():
-        r, k = iota((384, 288), 0), iota((384, 288), 1)
+        r, k = iota((384, 304), 0), iota((384, 304), 1)
         block, j, i = r // 48, (r % 48) // 8, r % 8
-        spread[...] = ((k % 8 == block) & (k // 8 == i * 6 + j) & (i < 6)).astype(F32).astype(BF16)
+        source = jnp.where(i < 6, (i * 6 + j) * 8 + block, jnp.where((i == 6) & (j == 0), 288 + block, -1))
+        spread[...] = (k == source).astype(F32).astype(BF16)
         for d in first[:3]:
             d.wait()
 
-    greet([dev(x + 1, y, z, c), dev(x + 3, y, z, c), dev(x, y + 1, z, c), dev(x, y + 3, z, c), dev(x, y + 2, z, c), dev(x, y, z + 1, c), dev(x, y, z + 3, c), sib], between)
+    greet([dev(x + s, y, z, c) for s in (1, 2, 3)] + [dev(x, y + s, z, c) for s in (1, 2, 3)] + [dev(x, y, z + s, c) for s in (1, 2, 3)] + [sib], between)
     sends = []
 
     def send(src, dst, recv, device):
@@ -288,72 +287,66 @@
     def arrive(dst, recv):
         pltpu.make_async_remote_copy(src_ref=dst, dst_ref=dst, send_sem=s_send.at[0], recv_sem=recv, device_id=sib, device_id_type=MESH).wait_recv()
 
-    def slot(ref, xx, yy, cc=None):
-        return ref.at[index(xx, yy, cc)]
-
     written = []
 
-    def widen(ref, at, buf, out, sem):
-        got = ref[at]
-        buf[at] = jnp.dot(spread[...], got[0:288], preferred_element_type=F32).astype(BF16)
-        d = pltpu.make_async_copy(buf.at[at], out.at[at], sem.at[at])
+    def across(buf, out, sem, over, yy, xx):
+        send(buf.at[yy, xx], out.at[c, yy, xx], over.at[yy, xx], sib)
+        d = pltpu.make_async_copy(buf.at[yy, xx], out.at[c, yy, xx], sem.at[yy, xx])
         d.start()
         written.append(d)
 
-    def wide_of_q(xx, yy, cc=None):
-        widen(bq, index(xx, yy, cc), wq, wide_q, s_wq)
-
-    def wide_of_p(xx, yy, cc=None):
-        widen(bp, index(xx, yy, cc), wp, wide_p, s_wp)
-
-    own_piece = slot(bq, x, y)
-    for s in (1, 3):
+    def widen(yq, xq, yp, xp):
+        two = jnp.concatenate([bq[yq, xq], bp[yp, xp]], axis=1)
+        got = jnp.dot(spread[...], two, preferred_element_type=F32).astype(BF16)
+        wq[yq, xq] = got[:, :128]
+        wp[yp, xp] = got[:, 128:]
+        across(wq, wide_q, s_wq, s_as, yq, xq)
+        across(wp, wide_p, s_wp, s_bs, yp, xp)
+
+    peers = (1, 3, 2)
+    for s in peers:
         send(own_piece, stage.at[z], s_z.at[z], dev(x, y, z + s, c))
-        send(dall.at[z], dall.at[z], s_d.at[z], dev(x, y, z + s, c))
-    for s in (1, 3):
+    for s in peers if XDIRECT else (1, 3):
         send(own_piece, own_piece, s_ax.at[x], dev(x + s, y, z, c))
     for s in (1, 3):
-        send(own_piece, own_piece, s_ay.at[x, y], dev(x, y + s, z, c))
-    send(own_piece, own_piece, s_as.at[x, y], sib)
+        send(own_piece, own_piece, s_ay.at[y, x], dev(x, y + s, z, c))
+    for s in peers:
+        send(dall.at[z], dall.at[z], s_d.at[z], dev(x, y, z + s, c))
     keep = pltpu.make_async_copy(own_piece, stage.at[z], s_loc.at[0])
     keep.start()
-    wide_of_q(x, y)
-    zf = r4(z - way)
-    arrive(stage.at[zf], s_z.at[zf])
-    send(stage.at[zf], stage.at[zf], s_z.at[zf], dev(x, y, z + way, c))
-    arrive(dall.at[zf], s_d.at[zf])
-    send(dall.at[zf], dall.at[zf], s_d.at[zf], dev(x, y, z + way, c))
-
-    def spread_y(xx):
+    for s in peers:
+        arrive(stage.at[r4(z + s)], s_z.at[r4(z + s)])
+    keep.wait()
+    for s in peers:
+        yt = r4(y + s)
+        send(stage.at[yt], bp.at[y, x], s_by.at[y], dev(x, yt, z, c))
+    mine = pltpu.make_async_copy(stage.at[y], bp.at[y, x], s_loc.at[1])
+    mine.start()
+    for s in (1, 3):
+        send(stage.at[y], bp.at[y, x], s_bx.at[y, x], dev(x + s, y, z, c))
+
+    xf, xb, x2 = r4(x - way), r4(x + way), r4(x + 2)
+    yf, yb, y2 = r4(y - way), r4(y + way), r4(y + 2)
+    for xx in (xf, xb, x2):
+        arrive(bq.at[y, xx], s_ax.at[xx])
+        if not XDIRECT and xx is xf:
+            send(bq.at[y, xx], bq.at[y, xx], s_ax.at[xx], dev(x + way, y, z, c))
         for s in (1, 3):
-            send(slot(bq, xx, y), slot(bq, xx, y), s_ay.at[r4(xx), y], dev(x, y + s, z, c))
-        send(slot(bq, xx, y), slot(bq, xx, y), s_as.at[r4(xx), y], sib)
-
-    xf, xb = r4(x - way), r4(x + way)
-    arrive(slot(bq, xf, y), s_ax.at[xf])
-    send(slot(bq, xf, y), slot(bq, xf, y), s_ax.at[xf], dev(x + way, y, z, c))
-    spread_y(xf)
-    arrive(slot(bq, xb, y), s_ax.at[xb])
-    spread_y(xb)
-    for zz in (r4(z + way), r4(z + 2)):
-        arrive(stage.at[zz], s_z.at[zz])
-        arrive(dall.at[zz], s_d.at[zz])
-    keep.wait()
-    for s in (1, 3, 2):
-        yt = r4(y + s)
-        send(stage.at[yt], slot(bp, x, y), s_by.at[y], dev(x, yt, z, c))
-    mine = pltpu.make_async_copy(stage.at[y], slot(bp, x, y), s_loc.at[1])
-    mine.start()
-
-    def spread_x(src, yy):
+            send(bq.at[y, xx], bq.at[y, xx], s_ay.at[y, xx], dev(x, y + s, z, c))
+    for yy in (yf, yb, y2):
+        arrive(bp.at[yy, x], s_by.at[yy])
         for s in (1, 3):
-            send(src, slot(bp, x, yy), s_bx.at[x, r4(yy)], dev(x + s, y, z, c))
-        send(src, slot(bp, x, yy), s_bs.at[x, r4(yy)], sib)
-
-    spread_x(stage.at[y], y)
-    x2 = r4(x + 2)
-    arrive(slot(bq, x2, y), s_ax.at[x2])
-    spread_y(x2)
+            send(bp.at[yy, x], bp.at[yy, x], s_bx.at[yy, x], dev(x + s, y, z, c))
+    mine.wait()
+    widen(y, x, y, x)
+    for xx, yy in ((x, y), (xf, yf), (xb, yb), (x2, y2)):
+        arrive(bq.at[yf, xx], s_ay.at[yf, xx])
+        send(bq.at[yf, xx], bq.at[yf, xx], s_ay.at[yf, xx], dev(x, y + way, z, c))
+        arrive(bp.at[yy, xf], s_bx.at[yy, xf])
+        send(bp.at[yy, xf], bp.at[yy, xf], s_bx.at[yy, xf], dev(x + way, y, z, c))
+        if xx is not x:
+            widen(y, xx, yy, x)
+        widen(yf, xx, yy, xf)
     first[3].wait()
     parity = lax.rem(m, 2)
     vbuf[0:128] = held[pl.ds(pl.multiple_of(64 * parity, 64), 128), :]
@@ -365,11 +358,8 @@
         vt[q] = lax.dot_general(same, vbuf[:, 128 * q:128 * q + 128], NT, preferred_element_type=F32).astype(BF16)
     vt_copy = pltpu.make_async_copy(vt, vt_out, s_loc.at[2])
     vt_copy.start()
-    for s in (1, 3, 2):
-        yy = r4(y + s)
-        arrive(slot(bp, x, yy), s_by.at[yy])
-        spread_x(slot(bp, x, yy), yy)
-    mine.wait()
+    for s in peers:
+        arrive(dall.at[r4(z + s)], s_d.at[r4(z + s)])
     same = (iota((192, 192), 0) == iota((192, 192), 1)).astype(F32).astype(BF16)
     full = jnp.concatenate([dall[k] for k in range(4)], axis=0)
     turned = lax.dot_general(same, full, NT, preferred_element_type=F32).astype(BF16)
@@ -380,42 +370,16 @@
         dexp[l] = jnp.dot(turned, sel, preferred_element_type=F32)
     dexp_copy = pltpu.make_async_copy(dexp, dexp_out, s_loc.at[0])
     dexp_copy.start()
-    for xx in (xf, xb, x2):
-        wide_of_q(xx, y)
-    yf = r4(y - way)
-    for xx, yy in ((x, y), (xf, r4(y + 1)), (xb, r4(y + 3)), (x2, r4(y + 2))):
-        arrive(slot(bq, xx, yf), s_ay.at[xx, yf])
-        send(slot(bq, xx, yf), slot(bq, xx, yf), s_ay.at[xx, yf], dev(x, y + way, z, c))
-        send(slot(bq, xx, yf), slot(bq, xx, yf), s_as.at[xx, yf], sib)
-        arrive(slot(bp, xf, yy), s_bx.at[xf, yy])
-        send(slot(bp, xf, yy), slot(bp, xf, yy), s_bx.at[xf, yy], dev(x + way, y, z, c))
-        send(slot(bp, xf, yy), slot(bp, xf, yy), s_bs.at[xf, yy], sib)
-        wide_of_p(x, yy)
-        wide_of_q(xx, yf)
-        wide_of_p(xf, yy)
-    yb, y2 = r4(y + way), r4(y + 2)
     for ya, xa in ((yb, xb), (y2, x2)):
-        for s in range(4):
-            xx, yy = r4(x + s), r4(y + s)
-            arrive(slot(bq, xx, ya), s_ay.at[xx, ya])
-            send(slot(bq, xx, ya), slot(bq, xx, ya), s_as.at[xx, ya], sib)
-            arrive(slot(bp, xa, yy), s_bx.at[xa, yy])
-            send(slot(bp, xa, yy), slot(bp, xa, yy), s_bs.at[xa, yy], sib)
-            wide_of_q(xx, ya)
-            wide_of_p(xa, yy)
-    for xx, xp in ((x, x), (xf, xf), (xb, xb), (x2, x2)):
-        for yy in (y, yf, yb, y2):
-            arrive(slot(bq, xx, yy, o), s_as.at[xx, yy])
-            wide_of_q(xx, yy, o)
-            arrive(slot(bp, xx, yy, o), s_bs.at[xx, yy])
-            wide_of_p(xx, yy, o)
-    last = [
-        pltpu.make_async_copy(bq.at[:, 288:304], names_q, s_loc.at[1]),
-        pltpu.make_async_copy(bp.at[:, 288:304], names_p, s_loc.at[3]),
-    ]
-    for d in last:
-        d.start()
-    for d in written + last + [vt_copy, dexp_copy]:
+        for xx, yy in ((x, y), (xf, yf), (xb, yb), (x2, y2)):
+            arrive(bq.at[ya, xx], s_ay.at[ya, xx])
+            arrive(bp.at[yy, xa], s_bx.at[yy, xa])
+            widen(ya, xx, yy, xa)
+    for yy in (y, yf, yb, y2):
+        for xx in (x, xf, xb, x2):
+            arrive(wide_q.at[o, yy, xx], s_as.at[yy, xx])
+            arrive(wide_p.at[o, yy, xx], s_bs.at[yy, xx])
+    for d in written + [vt_copy, dexp_copy]:
         d.wait()
     for d in sends:
         d.wait_send()
@@ -427,28 +391,26 @@
     return pl.pallas_call(
         gather_kernel,
         out_shape=[
-            jax.ShapeDtypeStruct((32, 384, 128), BF16),
-            jax.ShapeDtypeStruct((32, 384, 128), BF16),
-            jax.ShapeDtypeStruct((32, 16, 128), BF16),
-            jax.ShapeDtypeStruct((32, 16, 128), BF16),
+            jax.ShapeDtypeStruct((2, 4, 4, 384, 128), BF16),
+            jax.ShapeDtypeStruct((2, 4, 4, 384, 128), BF16),
             jax.ShapeDtypeStruct((12, 128, 256), BF16),
             jax.ShapeDtypeStruct((32, 192, 128), F32),
         ],
         in_specs=[hbm] * 4,
-        out_specs=[hbm] * 6,
+        out_specs=[hbm] * 4,
         scratch_shapes=[
-            pltpu.VMEM((32, ROWS, 128), BF16),
-            pltpu.VMEM((32, ROWS, 128), BF16),
+            pltpu.VMEM((4, 4, ROWS, 128), BF16),
+            pltpu.VMEM((4, 4, ROWS, 128), BF16),
             pltpu.VMEM((4, ROWS, 128), BF16),
             pltpu.VMEM((4, 48, 192), BF16),
             pltpu.VMEM((192, 1536), BF16),
             pltpu.VMEM((256, 1536), BF16),
             pltpu.VMEM((12, 128, 256), BF16),
             pltpu.VMEM((32, 192, 128), F32),
-            pltpu.VMEM((32, 384, 128), BF16),
-            pltpu.VMEM((32, 384, 128), BF16),
-            pltpu.VMEM((384, 288), BF16),
-            dma((72,)), dma((4,)), dma((4,)), dma((4,)), dma((4, 4)), dma((4, 4)), dma((4,)), dma((4, 4)), dma((4, 4)), dma((4,)), dma((32,)), dma((32,)),
+            pltpu.VMEM((4, 4, 384, 128), BF16),
+            pltpu.VMEM((4, 4, 384, 128), BF16),
+            pltpu.VMEM((384, 304), BF16),
+            dma((80,)), dma((4,)), dma((4,)), dma((4,)), dma((4, 4)), dma((4, 4)), dma((4,)), dma((4, 4)), dma((4, 4)), dma((4,)), dma((4, 4)), dma((4, 4)),
         ],
         compiler_params=pltpu.CompilerParams(collective_id=0, has_side_effects=True, vmem_limit_bytes=48 << 20),
         name="gather",
@@ -520,12 +482,13 @@
     parity, chip = m % 2, m // 2
     names = jnp.pad(block_list.astype(BF16), ((0, 8), (0, 125)))
     own = block_values.transpose(1, 2, 0, 3).reshape(288, 128)
-    bq, bp, names_q, names_p, vt, dexp = gather(own, names, density, metric_inverse)
+    bq, bp, vt, dexp = gather(own, names, density, metric_inverse)
+    bq, bp = bq.reshape(256, 48, 128), bp.reshape(256, 48, 128)
 
     def lists(b):
-        return b[:, :8, :3].reshape(256, 3).astype(I32)
-    codex, codep, meta, sig = tables(lists(names_q), lists(names_p), atom_offsets // 6, 3 * chip + 2 * parity, 3 * chip + 1, r * 12, parity)
-    part = contract(codex, codep, meta, sig, bq.reshape(256, 48, 128), bp.reshape(256, 48, 128), vt, dexp)
+        return b[:, 6, :3].astype(I32)
+    codex, codep, meta, sig = tables(lists(bq), lists(bp), atom_offsets // 6, 3 * chip + 2 * parity, 3 * chip + 1, r * 12, parity)
+    part = contract(codex, codep, meta, sig, bq, bp, vt, dexp)
     return reduce(part.reshape(4, 8, 8, 256))[:6, :48]
 
 

time: 108 us -> 112 us (1.037)
  Pallas kernels: 91.4 us -> 95.5 us
  local copies, waits for them, and re-layouts: 11.1 us -> 8.86 us
  other arithmetic: 5.33 us -> 7.43 us
    pallas_call x1, Pallas kernels: 22.9 us -> 35.7 us  [reduce(): pl.pallas_call(reduce_kernel, out_shape=jax.ShapeDtypeStruct((8, 128), F3...]
    pallas_call x1, Pallas kernels: 41.3 us -> 34.4 us  [gather(): pl.pallas_call(gather_kernel, out_shape=[jax.ShapeDtypeStruct((2, 4, 4, 3...]
    unnamed x17 -> x11, local copies, waits for them, and re-layouts: 7.01 us -> 4.84 us
    convert_element_type x1 -> x2, other arithmetic: 0.03 us -> 1.89 us  [lists(): return b[:, 6, :3].astype(I32)]
    pallas_call x1, Pallas kernels: 27.2 us -> 25.4 us  [contract(): pl.pallas_call(contract_kernel, out_shape=jax.ShapeDtypeStruct((256, 256)...]
where the time goes in v4:
time: 112 us
  Pallas kernels  95.5 us (85%)
  local copies, waits for them, and re-layouts  8.86 us (8%)
  other arithmetic  7.43 us (7%)
    pallas_call x1, Pallas kernels, reduce(): pl.pallas_call(reduce_kernel, out_shape=jax.ShapeDtypeStruct((8, 128), F3...  35.7 us
    pallas_call x1, Pallas kernels, gather(): pl.pallas_call(gather_kernel, out_shape=[jax.ShapeDtypeStruct((2, 4, 4, 3...  34.4 us
    pallas_call x1, Pallas kernels, contract(): pl.pallas_call(contract_kernel, out_shape=jax.ShapeDtypeStruct((256, 256)...  25.4 us
    unnamed x11, local copies, waits for them, and re-layouts  4.84 us
    concatenate x1, local copies, waits for them, and re-layouts, tables(): jnp.concatenate([starts, counts, ends[11:], jnp.stack([parity] * 4).astyp...  2.55 us

profile of v4, /device:TPU:1, one launch (start us, length us, event | category | flops | bytes accessed | tf_op | source)
XLA Modules:
  0.0 111.9 jit_solution(486458970540309356)
XLA Ops:
  0.0 0.7 and_select_fusion
  0.7 0.7 convert_element_type.47
  1.4 0.1 copy.9
  1.5 0.0 copy-start.2
  1.5 1.1 copy-done.2
  2.5 0.0 copy-start.3
  2.5 0.9 copy-done.3
  3.4 0.0 copy-start.4
  3.4 0.7 copy-done.4
  4.2 34.4 %gather.1 = (bf16[2,4,4,384,128]{4,3,2,1,0:T(8,128)(2,1)S(1)}, bf16[2,4,4,384,128]{4,3,2,1,0:T(8,128)(2,1)}, bf16[12,128,256]{2,1,0:T(8,128)(2,1)S(1)}, f32[32,192,128]{2,1,0:T(8,128)}) custom-call(bf16[288,128]{1,0:T(8,128)(2,1)S(1)} %bitcast.27, bf16[16,128]{1,0:T(8,128)(2,1)S(1)} %pad.4.names, bf16[48,192]{1,0:T(8,128)(2,1)S(1)} %copy-done.4, ...), custom_call_target="tpu_custom_call" | custom-call | tf_op jit(solution)/shard_map/gather/pallas_call | solution.py:391
  38.6 0.0 copy-start.1
  38.6 0.9 copy-done.1
  39.5 0.0 copy-start
  39.5 1.7 %slice_convert_fusion = s32[256,1,3]{2,1,0:T(1,128)S(1)} fusion(bf16[256,48,128]{2,1,0:T(8,128)(2,1)} %bitcast.28), kind=kLoop, calls=%fused_computation.21 | loop fusion | flops 768 | bytes 4608 | tf_op jit(solution)/shard_map/convert_element_type | solution.py:489
  41.1 0.2 slice_convert_fusion.1
  41.4 0.4 slice_reduce_fusion
  41.8 0.1 select_reduce_fusion.4
  41.9 0.1 convert_reduce_fusion.3
  42.0 0.2 convert_reduce_fusion.1
  42.2 0.1 select_reduce_fusion.1
  42.4 0.2 convert_reduce_fusion.4
  42.6 0.2 reduce-window.4
  42.8 0.7 slice.46
  43.4 0.1 convert_reduce_fusion.6
  43.5 0.1 add_subtract_fusion
  43.6 0.1 select_reduce_fusion.8
  43.7 0.2 convert_reduce_fusion
  43.9 0.6 select_reduce_fusion.2.codep
  44.5 0.7 fusion.8
  45.2 2.6 %concatenate.14.meta = s32[84]{0:T(128)} concatenate(s32[33]{0:T(128)S(1)} %convert_reduce_fusion.3, s32[1]{0:T(128)} %bitcast.9, s32[1]{0:T(128)} %bitcast.10, s32[1]{0:T(128)} %bitcast.11, s32[1]{0:T(128)} %bitcast.12, s32[1]{0:T(128)} %bitcast.12, s32[1]{0:T(128)} %bitcast.12, s32[1]{0:T(128)} %bitcast.12, s32[44]{0:T(128)S(1)} %broadcast_minimum_fusion), dimensions={0} | concatenate | bytes 672 | tf_op jit(solution)/shard_map/concatenate | solution.py:222
  47.7 0.2 fusion
  48.0 0.1 select_reduce_fusion
  48.1 0.6 broadcast_add_fusion.codex
  48.7 0.1 add_select_fusion
  48.8 0.7 select_n.109.sig
  49.5 0.0 copy-done
  49.5 25.4 %contract.1 = f32[256,256]{1,0:T(8,128)} custom-call(s32[352]{0:T(512)} %broadcast_add_fusion.codex, s32[256]{0:T(256)} %select_reduce_fusion.2.codep, s32[84]{0:T(128)} %concatenate.14.meta, s32[1,2048]{1,0:T(1,128)} %select_n.109.sig, bf16[256,48,128]{2,1,0:T(8,128)(2,1)} %bitcast.26, bf16[256,48,128]{2,1,0:T(8,128)(2,1)} %bitcast.29, ...), custom_call_target="tpu_custom_call" | custom-call | tf_op jit(solution)/shard_map/contract/pallas_call | solution.py:169
  75.0 35.7 %reduce.13 = f32[8,128]{1,0:T(8,128)} custom-call(f32[4,8,8,256]{3,2,1,0:T(8,128)} %bitcast.32), custom_call_target="tpu_custom_call" | custom-call | tf_op jit(solution)/shard_map/reduce/pallas_call | solution.py:464
  110.6 1.3 %copy.11 = f32[6,48]{1,0:T(8,128)} copy(f32[6,48]{1,0:T(8,128)} %bitcast.33) | data formatting | bytes 2304
  (10 shorter events, 0.1 us)
Async XLA Ops:
  1.5 1.1 copy-start.2
  2.5 0.9 copy-start.3
  3.4 0.7 copy-start.4
  38.6 0.9 copy-start.1
  39.5 10.0 %copy-start = (bf16[2,4,4,384,128]{4,3,2,1,0:T(8,128)(2,1)}, bf16[2,4,4,384,128]{4,3,2,1,0:T(8,128)(2,1)S(1)}, u32[]{:S(2)}) copy-start(bf16[2,4,4,384,128]{4,3,2,1,0:T(8,128)(2,1)S(1)} %get-tuple-element.9) | copy-start | bytes 9437188

commit v5 on v4

--- a/solution.py
+++ b/solution.py
@@ -22,12 +22,12 @@
 
 
 def contract_kernel(codex, codep, meta, sig, bq, bp_hbm, vt, dexp_hbm, out, xbuf, hbuf, obuf, sbuf, ebuf, kbuf, bp, dexp, s_b, s_d):
-    nf, nh = meta[33], meta[34]
+    nf, nh = meta[0, 33], meta[0, 34]
     table = pltpu.make_async_copy(dexp_hbm, dexp, s_d.at[0])
     table.start()
 
     def fetch(t):
-        return pltpu.make_async_copy(bp_hbm.at[codep[t] & 255], bp.at[t, 0:48], s_b.at[t])
+        return pltpu.make_async_copy(bp_hbm.at[codep[0, t] & 255], bp.at[t, 0:48], s_b.at[t])
 
     def f_step(t, carry):
         fetch(t).start()
@@ -40,9 +40,9 @@
     def x_step(step, carry):
         for w in range(XUN):
             ch = XUN * step + w
-            src = [codex[8 * ch + u] for u in range(8)]
+            src = [codex[0, 8 * ch + u] for u in range(8)]
             rows = jnp.concatenate([bq[s & 255] for s in src], axis=0)
-            x = jnp.dot(rows, vt[meta[40 + ch]], preferred_element_type=F32)
+            x = jnp.dot(rows, vt[meta[0, 40 + ch]], preferred_element_type=F32)
             for u in range(8):
                 tiles = [x[48 * u + 8 * j:48 * u + 8 * j + 8] for j in range(6)]
                 whole = [t[:, :128] for t in tiles]
@@ -50,7 +50,7 @@
                 xbuf[src[u] >> 8] = jnp.stack(whole + half)
         return carry
 
-    lax.fori_loop(0, (meta[35] + XUN - 1) // XUN, x_step, 0)
+    lax.fori_loop(0, (meta[0, 35] + XUN - 1) // XUN, x_step, 0)
     kbuf[...] = jnp.zeros_like(kbuf)
     ebuf[...] = jnp.zeros_like(ebuf)
     sbuf[...] = (iota((256, 2048), 0) == sig[...]).astype(F32).astype(BF16)
@@ -58,7 +58,7 @@
     low_mask = (lane % 8 == sub) & (lane < 64)
     high_mask = (lane % 8 == sub) & (lane >= 64)
     row, col = iota((8, 256), 0), iota((8, 256), 1)
-    even_device = (iota((64, 128), 0) * 0 + meta[36]) == 0
+    even_device = (iota((64, 128), 0) * 0 + meta[0, 36]) == 0
     left_lanes = iota((64, 128), 1) < 64
     none = jnp.zeros((64, 128), BF16)
     table.wait()
@@ -84,7 +84,7 @@
             at, ls = [], []
             for u in range(2):
                 t = base + jnp.minimum(2 * t2 + u, cnt - 1)
-                code = codep[t]
+                code = codep[0, t]
                 at.append(t)
                 ls.append((code >> 8) & 31)
                 ebuf[pl.ds(pl.multiple_of(16 * t2 + 8 * u, 8), 8), :] = (col == 8 * (code >> 13) + row).astype(F32)
@@ -121,7 +121,7 @@
             obuf[pl.ds(pl.multiple_of(8 * k0, 8), CHUNK * 8), :] = o
 
         def n_step(i, carry):
-            ends = [meta[NB * i + u] for u in range(NB + 1)]
+            ends = [meta[0, NB * i + u] for u in range(NB + 1)]
             for u in range(NB):
                 chunk(NB * i + u, ends[u])
             longest = ends[1] - ends[0]
@@ -131,7 +131,7 @@
             @pl.when(longest > CHUNK)
             def _():
                 def again(n, carry):
-                    s0, s1 = meta[n], meta[n + 1]
+                    s0, s1 = meta[0, n], meta[0, n + 1]
 
                     def c_step(c, carry):
                         chunk(n, s0 + CHUNK * c)
@@ -183,47 +183,12 @@
             pltpu.SemaphoreType.DMA((256,)),
             pltpu.SemaphoreType.DMA((1,)),
         ],
-        compiler_params=pltpu.CompilerParams(vmem_limit_bytes=60 << 20),
+        compiler_params=pltpu.CompilerParams(vmem_limit_bytes=62 << 20),
         name="contract",
     )(codex, codep, meta, sig, bq, bp, vt, dexp)
 
 
-def tables(listq, listp, slots, whole_block, half_block, row_start, parity):
-    at = jnp.arange(256, dtype=I32)
-
-    def slot(x):
-        return jnp.sum(jnp.where(x[:, None] == jnp.arange(32, dtype=I32), slots, 0), axis=1)
-
-    def count(keys, upto):
-        return jnp.sum((keys[None, :] < upto[:, None]).astype(I32), axis=1)
-
-    def rank(key):
-        before = (key[None, :] < key[:, None]) | ((key[None, :] == key[:, None]) & (at[None, :] < at[:, None]))
-        return jnp.sum(before.astype(I32), axis=1)
-
-    def place(where, n, code, rest):
-        hit = where[None, :] == jnp.arange(n, dtype=I32)[:, None]
-        return rest + jnp.sum(jnp.where(hit, code[None, :] - rest, 0), axis=1)
-
-    q = listq[:, 2] - row_start
-    by_n = rank(slot(listq[:, 1]))
-    starts = count(slot(listq[:, 1]), jnp.arange(33, dtype=I32))
-    sig = 6 * place(by_n, 256, slot(listq[:, 0]), 0)[:, None] + jnp.arange(8, dtype=I32)
-    sig = jnp.where(jnp.arange(8) < 6, sig, -1).reshape(1, 2048)
-    ends = jnp.cumsum((count(q, jnp.arange(1, 13, dtype=I32)) - count(q, jnp.arange(12, dtype=I32)) + 7) // 8)
-    lead = 8 * jnp.sum(jnp.where(q[:, None] > jnp.arange(12, dtype=I32), (ends - jnp.concatenate([ends[:1] * 0, ends[:-1]]))[None, :], 0), axis=1)
-    within = rank(q) - jnp.sum((q[None, :] < q[:, None]).astype(I32), axis=1)
-    codex = place(lead + within, 8 * XROWS, at + (by_n << 8), 256 << 8)
-    chunk_q = jnp.minimum(jnp.sum((ends[None, :] <= jnp.arange(XROWS, dtype=I32)[:, None]).astype(I32), axis=1), 11)
-    p = listp[:, 2]
-    keyp = jnp.where(p == whole_block, 0, jnp.where(p == half_block, 1, 2))
-    codep = place(rank(keyp), 256, at + (slot(listp[:, 1]) << 8) + (slot(listp[:, 0]) << 13), 0)
-    counts = jnp.stack([jnp.sum((keyp == 0).astype(I32)), jnp.sum((keyp == 1).astype(I32))])
-    meta = jnp.concatenate([starts, counts, ends[11:], jnp.stack([parity] * 4).astype(I32), chunk_q])
-    return codex, codep, meta, sig
-
-
-ROWS = 304
+ROWS = 288
 XDIRECT = True
 
 
@@ -245,7 +210,62 @@
     pl.semaphore_wait(barrier, len(devices))
 
 
-def gather_kernel(own, names, dens, v, wide_q, wide_p, vt_out, dexp_out, bq, bp, stage, dall, held, vbuf, vt, dexp, wq, wp, spread, s_send, s_z, s_d, s_ax, s_ay, s_as, s_by, s_bx, s_bs, s_loc, s_wq, s_wp):
+def tables(nq, nn, whole_block, half_block, row_start, parity, codex, codep, meta, sig):
+    g = iota((256, 1), 0)
+    wide = iota((256, 256), 1)
+    lane = iota((256, 128), 1)
+
+    def column(ref, field):
+        rows = []
+        for t in range(32):
+            c, s, u = t // 16, (t // 4) % 4, t % 4
+            rows.append(ref[c, s, u, pl.ds(field, 8, stride=0), :])
+        spread = jnp.concatenate(rows, axis=0)
+        return jnp.sum(jnp.where(lane == g % 8, spread, 0.0), axis=1, keepdims=True).astype(I32)
+
+    def across(col):
+        return jnp.sum(jnp.where(wide == g, col.astype(F32), 0.0), axis=0, keepdims=True).astype(I32)
+
+    def lanes(hit):
+        return jnp.sum(hit.astype(F32), axis=1, keepdims=True).astype(I32)
+
+    def rows(hit):
+        return jnp.sum(hit.astype(F32), axis=0, keepdims=True).astype(I32)
+
+    def rank(col):
+        other = across(col)
+        return lanes((other < col) | ((other == col) & (wide < g)))
+
+    def put(where, at, code, rest):
+        return rest + jnp.sum(jnp.where(where == at, (code - rest).astype(F32), 0.0), axis=0, keepdims=True).astype(I32)
+
+    first, second, q = column(nq, 0), column(nq, 1), column(nq, 2) - row_start
+    by_n = rank(second)
+    starts = rows(second < lane)
+    sig_at = iota((256, 2048), 1)
+    where = jnp.sum(jnp.where(by_n == sig_at // 8, first.astype(F32), 0.0), axis=0, keepdims=True).astype(I32)
+    inner = iota((1, 2048), 1) % 8
+    sig[...] = jnp.where(inner < 6, 6 * where + inner, -1)
+    other = across(q)
+    within = lanes((other == q) & (wide < g))
+    chunks_row = (rows(q == lane) + 7) // 8
+    n16, l16 = iota((16, 128), 0), iota((16, 128), 1)
+    ends_col = jnp.sum(jnp.where(l16 <= n16, chunks_row.astype(F32), 0.0), axis=1, keepdims=True).astype(I32)
+    lead = jnp.sum(jnp.where(lane < q, chunks_row.astype(F32), 0.0), axis=1, keepdims=True).astype(I32)
+    codex[...] = put(8 * lead + within, iota((256, 512), 1), g + by_n * 256, 256 * 256)
+    at128 = iota((1, 128), 1)
+    chunk_q = jnp.minimum(rows((ends_col <= l16 - 40) & (n16 < 12)), 11)
+    total = jnp.sum(chunks_row.astype(F32), axis=1, keepdims=True).astype(I32)
+    p = column(nn, 2)
+    key = jnp.where(p == whole_block, 0, jnp.where(p == half_block, 1, 2))
+    piece = g // 8
+    place_of = ((piece // 16) * 16 + (piece % 4) * 4 + (piece // 4) % 4) * 8 + g % 8
+    codep[...] = put(rank(key), wide, place_of + column(nn, 1) * 256 + column(nn, 0) * 8192, 0)
+    n0, n1 = rows(key == 0), rows(key == 1)
+    meta[...] = jnp.where(at128 < 33, starts, jnp.where(at128 == 33, n0, jnp.where(at128 == 34, n1, jnp.where(at128 == 35, total, jnp.where(at128 == 36, parity, jnp.where(at128 < 40, 0, chunk_q))))))
+
+
+def gather_kernel(own, triples, offsets, dens, v, wide_q, wide_p, vt_out, dexp_out, codex, codep, meta, sig, bq, bp, stage, dall, held, vbuf, vt, dexp, wq, wp, spread, s_send, s_z, s_d, s_ax, s_ay, s_as, s_by, s_bx, s_bs, s_loc, s_wq, s_wp, nq, nn, nz, s_nz, s_nx, s_ny, s_my, s_mx, s_ns):
     m, x, y, z, c = place()
     way = 1 - 2 * c
     o = 1 - c
@@ -259,8 +279,7 @@
     sib = dev(x, y, z, o)
     own_piece = bq.at[y, x]
     first = [
-        pltpu.make_async_copy(own, bq.at[y, x, 0:288], s_loc.at[0]),
-        pltpu.make_async_copy(names, bq.at[y, x, 288:304], s_loc.at[1]),
+        pltpu.make_async_copy(own, bq.at[y, x], s_loc.at[0]),
         pltpu.make_async_copy(dens, dall.at[z], s_loc.at[2]),
         pltpu.make_async_copy(v, held, s_loc.at[3]),
     ]
@@ -268,11 +287,18 @@
         d.start()
 
     def between():
-        r, k = iota((384, 304), 0), iota((384, 304), 1)
+        r, k = iota((384, 288), 0), iota((384, 288), 1)
         block, j, i = r // 48, (r % 48) // 8, r % 8
-        source = jnp.where(i < 6, (i * 6 + j) * 8 + block, jnp.where((i == 6) & (j == 0), 288 + block, -1))
+        source = jnp.where(i < 6, (i * 6 + j) * 8 + block, -1)
         spread[...] = (k == source).astype(F32).astype(BF16)
-        for d in first[:3]:
+        row, lane = iota((8, 128), 0), iota((8, 128), 1)
+        tile = jnp.zeros((8, 128), F32)
+        for k in range(8):
+            a, l, p = offsets[triples[0, k]] // 6, offsets[triples[1, k]] // 6, triples[2, k]
+            tile = jnp.where(lane == k, jnp.where(row == 0, a, jnp.where(row == 1, l, p)).astype(F32), tile)
+        nq[c, y, x] = tile
+        nz[z] = tile
+        for d in first[:2]:
             d.wait()
 
     greet([dev(x + s, y, z, c) for s in (1, 2, 3)] + [dev(x, y + s, z, c) for s in (1, 2, 3)] + [dev(x, y, z + s, c) for s in (1, 2, 3)] + [sib], between)
@@ -311,6 +337,9 @@
     for s in (1, 3):
         send(own_piece, own_piece, s_ay.at[y, x], dev(x, y + s, z, c))
     for s in peers:
+        send(nz.at[z], nz.at[z], s_nz.at[z], dev(x, y, z + s, c))
+        send(nq.at[c, y, x], nq.at[c, y, x], s_nx.at[x], dev(x + s, y, z, c))
+    for s in peers:
         send(dall.at[z], dall.at[z], s_d.at[z], dev(x, y, z + s, c))
     keep = pltpu.make_async_copy(own_piece, stage.at[z], s_loc.at[0])
     keep.start()
@@ -320,6 +349,12 @@
     for s in peers:
         yt = r4(y + s)
         send(stage.at[yt], bp.at[y, x], s_by.at[y], dev(x, yt, z, c))
+    for s in peers:
+        arrive(nz.at[r4(z + s)], s_nz.at[r4(z + s)])
+    nn[c, x, y] = nz[y]
+    for s in peers:
+        yt = r4(y + s)
+        send(nz.at[yt], nn.at[c, x, y], s_my.at[y], dev(x, yt, z, c))
     mine = pltpu.make_async_copy(stage.at[y], bp.at[y, x], s_loc.at[1])
     mine.start()
     for s in (1, 3):
@@ -333,10 +368,18 @@
             send(bq.at[y, xx], bq.at[y, xx], s_ax.at[xx], dev(x + way, y, z, c))
         for s in (1, 3):
             send(bq.at[y, xx], bq.at[y, xx], s_ay.at[y, xx], dev(x, y + s, z, c))
+    for xx in (xf, xb, x2):
+        arrive(nq.at[c, y, xx], s_nx.at[xx])
+    for s in peers:
+        send(nq.at[c, y], nq.at[c, y], s_ny.at[y], dev(x, y + s, z, c))
     for yy in (yf, yb, y2):
         arrive(bp.at[yy, x], s_by.at[yy])
         for s in (1, 3):
             send(bp.at[yy, x], bp.at[yy, x], s_bx.at[yy, x], dev(x + s, y, z, c))
+    for yy in (yf, yb, y2):
+        arrive(nn.at[c, x, yy], s_my.at[yy])
+    for s in peers:
+        send(nn.at[c, x], nn.at[c, x], s_mx.at[x], dev(x + s, y, z, c))
     mine.wait()
     widen(y, x, y, x)
     for xx, yy in ((x, y), (xf, yf), (xb, yb), (x2, y2)):
@@ -347,7 +390,12 @@
         if xx is not x:
             widen(y, xx, yy, x)
         widen(yf, xx, yy, xf)
-    first[3].wait()
+    for s in peers:
+        arrive(nq.at[c, r4(y + s)], s_ny.at[r4(y + s)])
+        arrive(nn.at[c, r4(x + s)], s_mx.at[r4(x + s)])
+    send(nq.at[c], nq.at[c], s_ns.at[0], sib)
+    send(nn.at[c], nn.at[c], s_ns.at[1], sib)
+    first[2].wait()
     parity = lax.rem(m, 2)
     vbuf[0:128] = held[pl.ds(pl.multiple_of(64 * parity, 64), 128), :]
     half = held[pl.ds(pl.multiple_of(128 * (1 - parity), 64), 64), :]
@@ -370,6 +418,10 @@
         dexp[l] = jnp.dot(turned, sel, preferred_element_type=F32)
     dexp_copy = pltpu.make_async_copy(dexp, dexp_out, s_loc.at[0])
     dexp_copy.start()
+    arrive(nq.at[o], s_ns.at[0])
+    arrive(nn.at[o], s_ns.at[1])
+    chip = m // 2
+    tables(nq, nn, 3 * chip + 2 * parity, 3 * chip + 1, z * 12, parity, codex, codep, meta, sig)
     for ya, xa in ((yb, xb), (y2, x2)):
         for xx, yy in ((x, y), (xf, yf), (xb, yb), (x2, y2)):
             arrive(bq.at[ya, xx], s_ay.at[ya, xx])
@@ -385,8 +437,10 @@
         d.wait_send()
 
 
-def gather(own, names, dens, v):
+def gather(own, triples, offsets, dens, v):
     hbm = pl.BlockSpec(memory_space=pl.ANY)
+    smem = pl.BlockSpec(memory_space=pltpu.SMEM)
+    vmem = pl.BlockSpec(memory_space=pltpu.VMEM)
     dma = pltpu.SemaphoreType.DMA
     return pl.pallas_call(
         gather_kernel,
@@ -395,9 +449,13 @@
             jax.ShapeDtypeStruct((2, 4, 4, 384, 128), BF16),
             jax.ShapeDtypeStruct((12, 128, 256), BF16),
             jax.ShapeDtypeStruct((32, 192, 128), F32),
+            jax.ShapeDtypeStruct((1, 512), I32),
+            jax.ShapeDtypeStruct((1, 256), I32),
+            jax.ShapeDtypeStruct((1, 128), I32),
+            jax.ShapeDtypeStruct((1, 2048), I32),
         ],
-        in_specs=[hbm] * 4,
-        out_specs=[hbm] * 4,
+        in_specs=[hbm, smem, smem, hbm, hbm],
+        out_specs=[hbm] * 4 + [vmem] * 4,
         scratch_shapes=[
             pltpu.VMEM((4, 4, ROWS, 128), BF16),
             pltpu.VMEM((4, 4, ROWS, 128), BF16),
@@ -409,12 +467,16 @@
             pltpu.VMEM((32, 192, 128), F32),
             pltpu.VMEM((4, 4, 384, 128), BF16),
             pltpu.VMEM((4, 4, 384, 128), BF16),
-            pltpu.VMEM((384, 304), BF16),
-            dma((80,)), dma((4,)), dma((4,)), dma((4,)), dma((4, 4)), dma((4, 4)), dma((4,)), dma((4, 4)), dma((4, 4)), dma((4,)), dma((4, 4)), dma((4, 4)),
+            pltpu.VMEM((384, 288), BF16),
+            dma((104,)), dma((4,)), dma((4,)), dma((4,)), dma((4, 4)), dma((4, 4)), dma((4,)), dma((4, 4)), dma((4, 4)), dma((4,)), dma((4, 4)), dma((4, 4)),
+            pltpu.VMEM((2, 4, 4, 8, 128), F32),
+            pltpu.VMEM((2, 4, 4, 8, 128), F32),
+            pltpu.VMEM((4, 8, 128), F32),
+            dma((4,)), dma((4,)), dma((4,)), dma((4,)), dma((4,)), dma((2,)),
         ],
-        compiler_params=pltpu.CompilerParams(collective_id=0, has_side_effects=True, vmem_limit_bytes=48 << 20),
+        compiler_params=pltpu.CompilerParams(collective_id=0, has_side_effects=True, vmem_limit_bytes=62 << 20),
         name="gather",
-    )(own, names, dens, v)
+    )(own, triples, offsets, dens, v)
 
 
 def reduce_kernel(part, out, got, cut, got2, send1, recv1, send2, recv2):
@@ -450,10 +512,11 @@
     got2[y, z] = cut[y, z]
     for yy, zz in far:
         pltpu.make_async_remote_copy(src_ref=cut.at[yy, zz], dst_ref=got2.at[yy, zz], send_sem=send2.at[0], recv_sem=recv2.at[yy, zz], device_id=(yy * 8 + g, zz), device_id_type=MESH).wait_recv()
-    result = got2[0, 0]
-    for k in range(1, 16):
-        result = result + got2[k // 4, k % 4]
-    out[...] = result
+    for part_of in range(2):
+        result = got2[2 * part_of, 0]
+        for k in range(1, 8):
+            result = result + got2[2 * part_of + k // 4, k % 4]
+        out[part_of] = result
     for cp in first + second:
         cp.wait_send()
 
@@ -463,7 +526,7 @@
     dma = pltpu.SemaphoreType.DMA
     return pl.pallas_call(
         reduce_kernel,
-        out_shape=jax.ShapeDtypeStruct((8, 128), F32),
+        out_shape=jax.ShapeDtypeStruct((2, 8, 128), F32),
         in_specs=[vmem],
         out_specs=vmem,
         scratch_shapes=[
@@ -478,18 +541,11 @@
 
 
 def body(block_list, block_values, atom_offsets, density, metric_inverse):
-    m, r = lax.axis_index("map"), lax.axis_index("row")
-    parity, chip = m % 2, m // 2
-    names = jnp.pad(block_list.astype(BF16), ((0, 8), (0, 125)))
     own = block_values.transpose(1, 2, 0, 3).reshape(288, 128)
-    bq, bp, vt, dexp = gather(own, names, density, metric_inverse)
-    bq, bp = bq.reshape(256, 48, 128), bp.reshape(256, 48, 128)
-
-    def lists(b):
-        return b[:, 6, :3].astype(I32)
-    codex, codep, meta, sig = tables(lists(bq), lists(bp), atom_offsets // 6, 3 * chip + 2 * parity, 3 * chip + 1, r * 12, parity)
-    part = contract(codex, codep, meta, sig, bq, bp, vt, dexp)
-    return reduce(part.reshape(4, 8, 8, 256))[:6, :48]
+    bq, bp, vt, dexp, codex, codep, meta, sig = gather(own, block_list.T, atom_offsets, density, metric_inverse)
+    part = contract(codex, codep, meta, sig, bq.reshape(256, 48, 128), bp.reshape(256, 48, 128), vt, dexp)
+    sums = reduce(part.reshape(4, 8, 8, 256))
+    return sums[0, :6, :48] + sums[1, :6, :48]
 
 
 def solution(mesh):

time: 112 us -> 80.3 us (0.72)
  Pallas kernels: 95.5 us -> 78.8 us
  local copies, waits for them, and re-layouts: 8.86 us -> 0 us
  other arithmetic: 7.43 us -> 1.27 us
    pallas_call x1, Pallas kernels: 35.7 us -> 17.1 us  [reduce(): pl.pallas_call(reduce_kernel, out_shape=jax.ShapeDtypeStruct((2, 8, 128),...]
    unnamed x11 -> x0, local copies, waits for them, and re-layouts: 4.84 us -> none
    reduce_sum x12 -> x0, other arithmetic: 2.74 us -> none  [the longest x3 0.91 us: place(): return rest + jnp.sum(jnp.where(hit, code[None, :] - rest, 0), axis=1)]
    convert_element_type x3 -> x0, other arithmetic: 2.58 us -> none  [the longest x2 1.89 us: lists(): return b[:, 6, :3].astype(I32)]
    concatenate x2 -> x0, local copies, waits for them, and re-layouts: 2.56 us -> none  [the longest x1 2.55 us: tables(): jnp.concatenate([starts, counts, ends[11:], jnp.stack([parity] * 4).astyp...]
where the time goes in v5:
time: 80.3 us; the launch traced here: 80.1 us
  Pallas kernels  78.8 us (98%)
  other arithmetic  1.27 us (2%)
    pallas_call x1, Pallas kernels, gather(): pl.pallas_call(gather_kernel, out_shape=[jax.ShapeDtypeStruct((2, 4, 4, 3...  35.4 us
    pallas_call x1, Pallas kernels, contract(): pl.pallas_call(contract_kernel, out_shape=jax.ShapeDtypeStruct((256, 256)...  26.3 us
    pallas_call x1, Pallas kernels, reduce(): pl.pallas_call(reduce_kernel, out_shape=jax.ShapeDtypeStruct((2, 8, 128),...  17.1 us

profile of v5, /device:TPU:1, one launch (start us, length us, event | category | flops | bytes accessed | tf_op | source)
XLA Modules:
  0.0 80.1 jit_solution(14893232109226664109)
XLA Ops:
  0.0 35.4 %gather.1 = (bf16[2,4,4,384,128]{4,3,2,1,0:T(8,128)(2,1)}, bf16[2,4,4,384,128]{4,3,2,1,0:T(8,128)(2,1)}, bf16[12,128,256]{2,1,0:T(8,128)(2,1)}, f32[32,192,128]{...) custom-call(bf16[288,128]{1,0:T(8,128)(2,1)} %bitcast.12, ...), custom_call_target="tpu_custom_call" | custom-call | tf_op jit(solution)/shard_map/gather/pallas_call | solution.py:445
  35.4 26.3 %contract.1 = f32[256,256]{1,0:T(8,128)} custom-call(s32[1,512]{1,0:T(1,128)} %get-tuple-element.13.codex, s32[1,256]{1,0:T(1,128)} %get-tuple-element.14.codep, s32[1,128]{1,0:T(1,128)} %get-tuple-element.15.meta, s32[1,2048]{1,0:T(1,128)} %get-tuple-element.16.sig, bf16[256,48,128]{2,1,0:T(8,128)(2,1)} %bitcast.9, bf16[256,48,128]{2,1,0:T(8,128)(2,1)} %bitcast.10, ...), custom_call_target="tpu_custom_call" | custom-call | tf_op jit(solution)/shard_map/contract/pallas_call | solution.py:169
  61.7 17.1 %reduce.1 = f32[2,8,128]{2,1,0:T(8,128)} custom-call(f32[4,8,8,256]{3,2,1,0:T(8,128)} %bitcast.11), custom_call_target="tpu_custom_call" | custom-call | tf_op jit(solution)/shard_map/reduce/pallas_call | solution.py:527
  78.8 1.3 %add_bitcast_fusion = f32[6,48]{1,0:T(8,128)} fusion(f32[2,8,128]{2,1,0:T(8,128)} %reduce.1), kind=kLoop, calls=%fused_computation | loop fusion | flops 288 | bytes 3456 | tf_op jit(solution)/shard_map/add | solution.py:548

commit v6 on v5

--- a/solution.py
+++ b/solution.py
@@ -21,20 +21,8 @@
     return lax.broadcasted_iota(I32, shape, axis)
 
 
-def contract_kernel(codex, codep, meta, sig, bq, bp_hbm, vt, dexp_hbm, out, xbuf, hbuf, obuf, sbuf, ebuf, kbuf, bp, dexp, s_b, s_d):
+def contract_kernel(codex, codep, meta, sig, bq, bp, vt, dexp, out, xbuf, hbuf, obuf, sbuf, ebuf, kbuf):
     nf, nh = meta[0, 33], meta[0, 34]
-    table = pltpu.make_async_copy(dexp_hbm, dexp, s_d.at[0])
-    table.start()
-
-    def fetch(t):
-        return pltpu.make_async_copy(bp_hbm.at[codep[0, t] & 255], bp.at[t, 0:48], s_b.at[t])
-
-    def f_step(t, carry):
-        fetch(t).start()
-        bp[t, 48:64] = jnp.zeros((16, 128), BF16)
-        return carry
-
-    lax.fori_loop(0, nf + nh, f_step, 0)
     low_half = iota((8, 128), 1) < 64
 
     def x_step(step, carry):
@@ -61,14 +49,6 @@
     even_device = (iota((64, 128), 0) * 0 + meta[0, 36]) == 0
     left_lanes = iota((64, 128), 1) < 64
     none = jnp.zeros((64, 128), BF16)
-    table.wait()
-
-    def w_step(t, carry):
-        fetch(t).wait()
-        return carry
-
-    lax.fori_loop(0, nf + nh, w_step, 0)
-
     def spread(ld, nu_a, lb, nu_b):
         a = dexp[ld, pl.ds(nu_a, 8, stride=0), :]
         b = dexp[lb, pl.ds(nu_b, 8, stride=0), :]
@@ -85,10 +65,10 @@
             for u in range(2):
                 t = base + jnp.minimum(2 * t2 + u, cnt - 1)
                 code = codep[0, t]
-                at.append(t)
+                at.append(code & 255)
                 ls.append((code >> 8) & 31)
                 ebuf[pl.ds(pl.multiple_of(16 * t2 + 8 * u, 8), 8), :] = (col == 8 * (code >> 13) + row).astype(F32)
-            b0, b1 = bp[at[0]], bp[at[1]]
+            b0, b1 = [jnp.concatenate([bp[k], none[:16]], axis=0) for k in at]
             if not half:
                 rhs = jnp.concatenate([jnp.concatenate([b0, none], axis=1), jnp.concatenate([none, b1], axis=1)], axis=0)
                 for c in range(0, 192, HN):
@@ -165,11 +145,10 @@
 def contract(codex, codep, meta, sig, bq, bp, vt, dexp):
     smem = pl.BlockSpec(memory_space=pltpu.SMEM)
     vmem = pl.BlockSpec(memory_space=pltpu.VMEM)
-    hbm = pl.BlockSpec(memory_space=pl.ANY)
     return pl.pallas_call(
         contract_kernel,
         out_shape=jax.ShapeDtypeStruct((256, 256), F32),
-        in_specs=[smem] * 3 + [vmem, vmem, hbm, vmem, hbm],
+        in_specs=[smem] * 3 + [vmem] * 5,
         out_specs=vmem,
         scratch_shapes=[
             pltpu.VMEM((256 + CHUNK, 9, 8, 128), F32),
@@ -178,12 +157,8 @@
             pltpu.VMEM((256, 2048), BF16),
             pltpu.VMEM((256, 256), F32),
             pltpu.VMEM((256, 256), F32),
-            pltpu.VMEM((256, 64, 128), BF16),
-            pltpu.VMEM((32, 192, 128), F32),
-            pltpu.SemaphoreType.DMA((256,)),
-            pltpu.SemaphoreType.DMA((1,)),
         ],
-        compiler_params=pltpu.CompilerParams(vmem_limit_bytes=62 << 20),
+        compiler_params=pltpu.CompilerParams(vmem_limit_bytes=36 << 20),
         name="contract",
     )(codex, codep, meta, sig, bq, bp, vt, dexp)
 
@@ -265,7 +240,7 @@
     meta[...] = jnp.where(at128 < 33, starts, jnp.where(at128 == 33, n0, jnp.where(at128 == 34, n1, jnp.where(at128 == 35, total, jnp.where(at128 == 36, parity, jnp.where(at128 < 40, 0, chunk_q))))))
 
 
-def gather_kernel(own, triples, offsets, dens, v, wide_q, wide_p, vt_out, dexp_out, codex, codep, meta, sig, bq, bp, stage, dall, held, vbuf, vt, dexp, wq, wp, spread, s_send, s_z, s_d, s_ax, s_ay, s_as, s_by, s_bx, s_bs, s_loc, s_wq, s_wp, nq, nn, nz, s_nz, s_nx, s_ny, s_my, s_mx, s_ns):
+def gather_kernel(own, triples, offsets, dens, v, wide_q, wide_p, vt_out, dexp_out, codex, codep, meta, sig, bq, bp, stage, dall, held, vbuf, spread, s_send, s_z, s_d, s_ax, s_ay, s_as, s_by, s_bx, s_bs, s_loc, nq, nn, nz, s_nz, s_nx, s_ny, s_my, s_mx, s_ns):
     m, x, y, z, c = place()
     way = 1 - 2 * c
     o = 1 - c
@@ -313,21 +288,13 @@
     def arrive(dst, recv):
         pltpu.make_async_remote_copy(src_ref=dst, dst_ref=dst, send_sem=s_send.at[0], recv_sem=recv, device_id=sib, device_id_type=MESH).wait_recv()
 
-    written = []
-
-    def across(buf, out, sem, over, yy, xx):
-        send(buf.at[yy, xx], out.at[c, yy, xx], over.at[yy, xx], sib)
-        d = pltpu.make_async_copy(buf.at[yy, xx], out.at[c, yy, xx], sem.at[yy, xx])
-        d.start()
-        written.append(d)
-
     def widen(yq, xq, yp, xp):
         two = jnp.concatenate([bq[yq, xq], bp[yp, xp]], axis=1)
         got = jnp.dot(spread[...], two, preferred_element_type=F32).astype(BF16)
-        wq[yq, xq] = got[:, :128]
-        wp[yp, xp] = got[:, 128:]
-        across(wq, wide_q, s_wq, s_as, yq, xq)
-        across(wp, wide_p, s_wp, s_bs, yp, xp)
+        wide_q[c, yq, xq] = got[:, :128]
+        wide_p[c, yp, xp] = got[:, 128:]
+        send(wide_q.at[c, yq, xq], wide_q.at[c, yq, xq], s_as.at[yq, xq], sib)
+        send(wide_p.at[c, yp, xp], wide_p.at[c, yp, xp], s_bs.at[yp, xp], sib)
 
     peers = (1, 3, 2)
     for s in peers:
@@ -403,9 +370,7 @@
     vbuf[192:256] = half
     same = (iota((128, 128), 0) == iota((128, 128), 1)).astype(F32).astype(BF16)
     for q in range(12):
-        vt[q] = lax.dot_general(same, vbuf[:, 128 * q:128 * q + 128], NT, preferred_element_type=F32).astype(BF16)
-    vt_copy = pltpu.make_async_copy(vt, vt_out, s_loc.at[2])
-    vt_copy.start()
+        vt_out[q] = lax.dot_general(same, vbuf[:, 128 * q:128 * q + 128], NT, preferred_element_type=F32).astype(BF16)
     for s in peers:
         arrive(dall.at[r4(z + s)], s_d.at[r4(z + s)])
     same = (iota((192, 192), 0) == iota((192, 192), 1)).astype(F32).astype(BF16)
@@ -415,9 +380,7 @@
     part = (lane % 64) // 8
     for l in range(32):
         sel = ((lam == 6 * l + part) & (part < 6)).astype(F32).astype(BF16)
-        dexp[l] = jnp.dot(turned, sel, preferred_element_type=F32)
-    dexp_copy = pltpu.make_async_copy(dexp, dexp_out, s_loc.at[0])
-    dexp_copy.start()
+        dexp_out[l] = jnp.dot(turned, sel, preferred_element_type=F32)
     arrive(nq.at[o], s_ns.at[0])
     arrive(nn.at[o], s_ns.at[1])
     chip = m // 2
@@ -431,14 +394,12 @@
         for xx in (x, xf, xb, x2):
             arrive(wide_q.at[o, yy, xx], s_as.at[yy, xx])
             arrive(wide_p.at[o, yy, xx], s_bs.at[yy, xx])
-    for d in written + [vt_copy, dexp_copy]:
-        d.wait()
     for d in sends:
         d.wait_send()
 
 
 def gather(own, triples, offsets, dens, v):
-    hbm = pl.BlockSpec(memory_space=pl.ANY)
+    hbm = pl.BlockSpec(memory_space=pltpu.HBM)
     smem = pl.BlockSpec(memory_space=pltpu.SMEM)
     vmem = pl.BlockSpec(memory_space=pltpu.VMEM)
     dma = pltpu.SemaphoreType.DMA
@@ -455,7 +416,7 @@
             jax.ShapeDtypeStruct((1, 2048), I32),
         ],
         in_specs=[hbm, smem, smem, hbm, hbm],
-        out_specs=[hbm] * 4 + [vmem] * 4,
+        out_specs=[vmem] * 8,
         scratch_shapes=[
             pltpu.VMEM((4, 4, ROWS, 128), BF16),
             pltpu.VMEM((4, 4, ROWS, 128), BF16),
@@ -463,18 +424,14 @@
             pltpu.VMEM((4, 48, 192), BF16),
             pltpu.VMEM((192, 1536), BF16),
             pltpu.VMEM((256, 1536), BF16),
-            pltpu.VMEM((12, 128, 256), BF16),
-            pltpu.VMEM((32, 192, 128), F32),
-            pltpu.VMEM((4, 4, 384, 128), BF16),
-            pltpu.VMEM((4, 4, 384, 128), BF16),
             pltpu.VMEM((384, 288), BF16),
-            dma((104,)), dma((4,)), dma((4,)), dma((4,)), dma((4, 4)), dma((4, 4)), dma((4,)), dma((4, 4)), dma((4, 4)), dma((4,)), dma((4, 4)), dma((4, 4)),
+            dma((104,)), dma((4,)), dma((4,)), dma((4,)), dma((4, 4)), dma((4, 4)), dma((4,)), dma((4, 4)), dma((4, 4)), dma((4,)),
             pltpu.VMEM((2, 4, 4, 8, 128), F32),
             pltpu.VMEM((2, 4, 4, 8, 128), F32),
             pltpu.VMEM((4, 8, 128), F32),
             dma((4,)), dma((4,)), dma((4,)), dma((4,)), dma((4,)), dma((2,)),
         ],
-        compiler_params=pltpu.CompilerParams(collective_id=0, has_side_effects=True, vmem_limit_bytes=62 << 20),
+        compiler_params=pltpu.CompilerParams(collective_id=0, has_side_effects=True, vmem_limit_bytes=24 << 20),
         name="gather",
     )(own, triples, offsets, dens, v)
 
@@ -535,14 +492,14 @@
             pltpu.VMEM((4, 4, 8, 128), F32),
             dma((8,)), dma((8,)), dma((16,)), dma((4, 4)),
         ],
-        compiler_params=pltpu.CompilerParams(collective_id=1, has_side_effects=True),
+        compiler_params=pltpu.CompilerParams(collective_id=1, has_side_effects=True, vmem_limit_bytes=8 << 20),
         name="reduce",
     )(part)
 
 
 def body(block_list, block_values, atom_offsets, density, metric_inverse):
     own = block_values.transpose(1, 2, 0, 3).reshape(288, 128)
-    bq, bp, vt, dexp, codex, codep, meta, sig = gather(own, block_list.T, atom_offsets, density, metric_inverse)
+    bq, bp, vt, dexp, codex, codep, meta, sig = gather(*[pltpu.with_memory_space_constraint(t, pltpu.HBM) for t in (own, block_list.T, atom_offsets, density, metric_inverse)])
     part = contract(codex, codep, meta, sig, bq.reshape(256, 48, 128), bp.reshape(256, 48, 128), vt, dexp)
     sums = reduce(part.reshape(4, 8, 8, 256))
     return sums[0, :6, :48] + sums[1, :6, :48]

time: 80.3 us -> 76.4 us (0.951)
  Pallas kernels: 78.8 us -> 75.7 us
    pallas_call x1, Pallas kernels: 26.3 us -> 21.2 us  [contract(): pl.pallas_call(contract_kernel, out_shape=jax.ShapeDtypeStruct((256, 256)...]
    pallas_call x1, Pallas kernels: 17.1 us -> 20.2 us  [reduce(): pl.pallas_call(reduce_kernel, out_shape=jax.ShapeDtypeStruct((2, 8, 128),...]
    pallas_call x1, Pallas kernels: 35.4 us -> 34.3 us  [gather(): pl.pallas_call(gather_kernel, out_shape=[jax.ShapeDtypeStruct((2, 4, 4, 3...]
where the time goes in v6:
time: 76.4 us; the launch traced here: 76.3 us
  Pallas kernels  75.7 us (99%)
    pallas_call x1, Pallas kernels, gather(): pl.pallas_call(gather_kernel, out_shape=[jax.ShapeDtypeStruct((2, 4, 4, 3...  34.3 us
    pallas_call x1, Pallas kernels, contract(): pl.pallas_call(contract_kernel, out_shape=jax.ShapeDtypeStruct((256, 256)...  21.2 us
    pallas_call x1, Pallas kernels, reduce(): pl.pallas_call(reduce_kernel, out_shape=jax.ShapeDtypeStruct((2, 8, 128),...  20.2 us

profile of v6, /device:TPU:1, one launch (start us, length us, event | category | flops | bytes accessed | tf_op | source)
XLA Modules:
  0.0 76.3 jit_solution(17094163275393706032)
XLA Ops:
  0.0 34.3 %gather.1 = (bf16[2,4,4,384,128]{4,3,2,1,0:T(8,128)(2,1)S(1)}, bf16[2,4,4,384,128]{4,3,2,1,0:T(8,128)(2,1)S(1)}, bf16[12,128,256]{2,1,0:T(8,128)(2,1)S(1)}, f32[...) custom-call(bf16[288,128]{1,0:T(8,128)(2,1)} %bitcast.12, ...), custom_call_target="tpu_custom_call" | custom-call | tf_op jit(solution)/shard_map/gather/pallas_call | solution.py:406
  34.3 21.2 %contract.1 = f32[256,256]{1,0:T(8,128)S(1)} custom-call(s32[1,512]{1,0:T(1,128)S(1)} %get-tuple-element.13.codex, s32[1,256]{1,0:T(1,128)S(1)} %get-tuple-element.14.codep, s32[1,128]{1,0:T(1,128)S(1)} %get-tuple-element.15.meta, s32[1,2048]{1,0:T(1,128)S(1)} %get-tuple-element.16.sig, bf16[256,48,128]{2,1,0:T(8,128)(2,1)S(1)} %bitcast.9, ...), custom_call_target="tpu_custom_call" | custom-call | tf_op jit(solution)/shard_map/contract/pallas_call | solution.py:148
  55.5 20.2 %reduce.1 = f32[2,8,128]{2,1,0:T(8,128)S(1)} custom-call(f32[4,8,8,256]{3,2,1,0:T(8,128)S(1)} %bitcast.11), custom_call_target="tpu_custom_call" | custom-call | tf_op jit(solution)/shard_map/reduce/pallas_call | solution.py:484
  75.7 0.6 add_bitcast_fusion

commit v7 on v6

--- a/solution.py
+++ b/solution.py
@@ -127,11 +127,13 @@
         for k in range(8):
             o = obuf[256 * k:256 * k + 256, :]
             high = o.astype(BF16)
-            low = (o - high.astype(F32)).astype(BF16)
             s = sbuf[:, 256 * k:256 * k + 256]
-            r += jnp.dot(s, high, preferred_element_type=F32) + jnp.dot(s, low, preferred_element_type=F32)
+            r += jnp.dot(s, high, preferred_element_type=F32)
         r = jnp.where(iota((256, 256), 1) < 8 * cnt, r, 0.0)
-        kbuf[...] += jnp.dot(r, ebuf[...], preferred_element_type=F32, precision=HI)
+        e = ebuf[...].astype(BF16)
+        high = r.astype(BF16)
+        low = (r - high.astype(F32)).astype(BF16)
+        kbuf[...] += jnp.dot(high, e, preferred_element_type=F32) + jnp.dot(low, e, preferred_element_type=F32)
 
     for half, base, total in ((False, 0, nf), (True, nf, nh)):
         def g_step(g, carry, half=half, base=base, total=total):
@@ -139,7 +141,7 @@
             return carry
 
         lax.fori_loop(0, (total + GROUP - 1) // GROUP, g_step, 0)
-    out[...] = kbuf[...].T
+    out[...] = kbuf[...].T.astype(BF16)
 
 
 def contract(codex, codep, meta, sig, bq, bp, vt, dexp):
@@ -147,7 +149,7 @@
     vmem = pl.BlockSpec(memory_space=pltpu.VMEM)
     return pl.pallas_call(
         contract_kernel,
-        out_shape=jax.ShapeDtypeStruct((256, 256), F32),
+        out_shape=jax.ShapeDtypeStruct((256, 256), BF16),
         in_specs=[smem] * 3 + [vmem] * 5,
         out_specs=vmem,
         scratch_shapes=[
@@ -240,7 +242,7 @@
     meta[...] = jnp.where(at128 < 33, starts, jnp.where(at128 == 33, n0, jnp.where(at128 == 34, n1, jnp.where(at128 == 35, total, jnp.where(at128 == 36, parity, jnp.where(at128 < 40, 0, chunk_q))))))
 
 
-def gather_kernel(own, triples, offsets, dens, v, wide_q, wide_p, vt_out, dexp_out, codex, codep, meta, sig, bq, bp, stage, dall, held, vbuf, spread, s_send, s_z, s_d, s_ax, s_ay, s_as, s_by, s_bx, s_bs, s_loc, nq, nn, nz, s_nz, s_nx, s_ny, s_my, s_mx, s_ns):
+def gather_kernel(own, triples, offsets, dens, v, wide_q, wide_p, vt_out, dexp_out, codex, codep, meta, sig, bq, bp, stage, dall, held, vbuf, spread, s_send, s_z, s_d, s_ax, s_ay, s_as, s_by, s_bx, s_bs, s_loc, nq, nn, nz, s_nz, s_nx, s_ny, s_my, s_mx, s_ns, s_plane):
     m, x, y, z, c = place()
     way = 1 - 2 * c
     o = 1 - c
@@ -297,6 +299,10 @@
         send(wide_p.at[c, yp, xp], wide_p.at[c, yp, xp], s_bs.at[yp, xp], sib)
 
     peers = (1, 3, 2)
+
+    def to_plane(src, zz, n):
+        return pltpu.make_async_remote_copy(src_ref=src, dst_ref=bp.at[y, x], send_sem=s_plane.at[n], recv_sem=s_by.at[y], device_id=dev(x, zz, z, c), device_id_type=MESH)
+
     for s in peers:
         send(own_piece, stage.at[z], s_z.at[z], dev(x, y, z + s, c))
     for s in peers if XDIRECT else (1, 3):
@@ -308,14 +314,21 @@
         send(nq.at[c, y, x], nq.at[c, y, x], s_nx.at[x], dev(x + s, y, z, c))
     for s in peers:
         send(dall.at[z], dall.at[z], s_d.at[z], dev(x, y, z + s, c))
+    @pl.when(z != y)
+    def _():
+        to_plane(own_piece, z, 0).start()
+
     keep = pltpu.make_async_copy(own_piece, stage.at[z], s_loc.at[0])
     keep.start()
-    for s in peers:
-        arrive(stage.at[r4(z + s)], s_z.at[r4(z + s)])
+    for n, s in enumerate(peers):
+        zz = r4(z + s)
+        arrive(stage.at[zz], s_z.at[zz])
+
+        @pl.when(zz != y)
+        def _(zz=zz, n=n):
+            to_plane(stage.at[zz], zz, n + 1).start()
+
     keep.wait()
-    for s in peers:
-        yt = r4(y + s)
-        send(stage.at[yt], bp.at[y, x], s_by.at[y], dev(x, yt, z, c))
     for s in peers:
         arrive(nz.at[r4(z + s)], s_nz.at[r4(z + s)])
     nn[c, x, y] = nz[y]
@@ -394,6 +407,13 @@
         for xx in (x, xf, xb, x2):
             arrive(wide_q.at[o, yy, xx], s_as.at[yy, xx])
             arrive(wide_p.at[o, yy, xx], s_bs.at[yy, xx])
+    for n, s in enumerate((0,) + peers):
+        zz = r4(z + s)
+
+        @pl.when(zz != y)
+        def _(zz=zz, n=n):
+            to_plane(own_piece if n == 0 else stage.at[zz], zz, n).wait_send()
+
     for d in sends:
         d.wait_send()
 
@@ -429,7 +449,7 @@
             pltpu.VMEM((2, 4, 4, 8, 128), F32),
             pltpu.VMEM((2, 4, 4, 8, 128), F32),
             pltpu.VMEM((4, 8, 128), F32),
-            dma((4,)), dma((4,)), dma((4,)), dma((4,)), dma((4,)), dma((2,)),
+            dma((4,)), dma((4,)), dma((4,)), dma((4,)), dma((4,)), dma((2,)), dma((4,)),
         ],
         compiler_params=pltpu.CompilerParams(collective_id=0, has_side_effects=True, vmem_limit_bytes=24 << 20),
         name="gather",
@@ -456,9 +476,9 @@
     for d in range(1, 8):
         gg = lax.rem(g + d, 8)
         pltpu.make_async_remote_copy(src_ref=part.at[:, gg], dst_ref=got.at[gg], send_sem=send1.at[d], recv_sem=recv1.at[gg], device_id=near[0], device_id_type=MESH).wait_recv()
-    total = got[0]
+    total = got[0].astype(F32)
     for k in range(1, 8):
-        total = total + got[k]
+        total = total + got[k].astype(F32)
     for zz in range(4):
         cut[:, zz, :, 0:48] = total[:, :, 48 * zz:48 * zz + 48]
     second = []
@@ -487,7 +507,7 @@
         in_specs=[vmem],
         out_specs=vmem,
         scratch_shapes=[
-            pltpu.VMEM((8, 4, 8, 256), F32),
+            pltpu.VMEM((8, 4, 8, 256), BF16),
             pltpu.VMEM((4, 4, 8, 128), F32),
             pltpu.VMEM((4, 4, 8, 128), F32),
             dma((8,)), dma((8,)), dma((16,)), dma((4, 4)),

time: 76.4 us -> 76.8 us (level)
    pallas_call x1, Pallas kernels: 20.2 us -> 23.7 us  [reduce(): pl.pallas_call(reduce_kernel, out_shape=jax.ShapeDtypeStruct((2, 8, 128),...]
    pallas_call x1, Pallas kernels: 34.3 us -> 32.6 us  [gather(): pl.pallas_call(gather_kernel, out_shape=[jax.ShapeDtypeStruct((2, 4, 4, 3...]
    pallas_call x1, Pallas kernels: 21.2 us -> 19.7 us  [contract(): pl.pallas_call(contract_kernel, out_shape=jax.ShapeDtypeStruct((256, 256)...]
where the time goes in v7:
time: 76.8 us; the launch traced here: 76.6 us
  Pallas kernels  76 us (99%)
    pallas_call x1, Pallas kernels, gather(): pl.pallas_call(gather_kernel, out_shape=[jax.ShapeDtypeStruct((2, 4, 4, 3...  32.6 us
    pallas_call x1, Pallas kernels, reduce(): pl.pallas_call(reduce_kernel, out_shape=jax.ShapeDtypeStruct((2, 8, 128),...  23.7 us
    pallas_call x1, Pallas kernels, contract(): pl.pallas_call(contract_kernel, out_shape=jax.ShapeDtypeStruct((256, 256)...  19.7 us

profile of v7, /device:TPU:1, one launch (start us, length us, event | category | flops | bytes accessed | tf_op | source)
XLA Modules:
  0.0 76.6 jit_solution(9498605667507717481)
XLA Ops:
  0.0 32.6 %gather.1 = (bf16[2,4,4,384,128]{4,3,2,1,0:T(8,128)(2,1)S(1)}, bf16[2,4,4,384,128]{4,3,2,1,0:T(8,128)(2,1)S(1)}, bf16[12,128,256]{2,1,0:T(8,128)(2,1)S(1)}, f32[...) custom-call(bf16[288,128]{1,0:T(8,128)(2,1)} %bitcast.12, ...), custom_call_target="tpu_custom_call" | custom-call | tf_op jit(solution)/shard_map/gather/pallas_call | solution.py:426
  32.6 19.7 %contract.1 = bf16[256,256]{1,0:T(8,128)(2,1)S(1)} custom-call(s32[1,512]{1,0:T(1,128)S(1)} %get-tuple-element.13.codex, s32[1,256]{1,0:T(1,128)S(1)} %get-tuple-element.14.codep, s32[1,128]{1,0:T(1,128)S(1)} %get-tuple-element.15.meta, s32[1,2048]{1,0:T(1,128)S(1)} %get-tuple-element.16.sig, bf16[256,48,128]{2,1,0:T(8,128)(2,1)S(1)} %bitcast.9, ...), custom_call_target="tpu_custom_call" | custom-call | tf_op jit(solution)/shard_map/contract/pallas_call | solution.py:150
  52.3 23.7 %reduce.1 = f32[2,8,128]{2,1,0:T(8,128)S(1)} custom-call(bf16[4,8,8,256]{3,2,1,0:T(8,128)(2,1)S(1)} %bitcast.11), custom_call_target="tpu_custom_call" | custom-call | tf_op jit(solution)/shard_map/reduce/pallas_call | solution.py:504
  76.0 0.6 add_bitcast_fusion

commit v8 on v7

--- a/solution.py
+++ b/solution.py
@@ -15,13 +15,14 @@
 XUN = 4
 HN = 48
 NB = 16
+HU = 2
 
 
 def iota(shape, axis):
     return lax.broadcasted_iota(I32, shape, axis)
 
 
-def contract_kernel(codex, codep, meta, sig, bq, bp, vt, dexp, out, xbuf, hbuf, obuf, sbuf, ebuf, kbuf):
+def contract_kernel(codex, codep, meta, sig, bq, bp, vt, dexp, out, xbuf, hbuf, obuf, ebuf, kbuf):
     nf, nh = meta[0, 33], meta[0, 34]
     low_half = iota((8, 128), 1) < 64
 
@@ -41,7 +42,6 @@
     lax.fori_loop(0, (meta[0, 35] + XUN - 1) // XUN, x_step, 0)
     kbuf[...] = jnp.zeros_like(kbuf)
     ebuf[...] = jnp.zeros_like(ebuf)
-    sbuf[...] = (iota((256, 2048), 0) == sig[...]).astype(F32).astype(BF16)
     lane, sub = iota((8, 128), 1), iota((8, 128), 0)
     low_mask = (lane % 8 == sub) & (lane < 64)
     high_mask = (lane % 8 == sub) & (lane >= 64)
@@ -60,7 +60,7 @@
         return both.astype(BF16)
 
     def group(half, base, cnt):
-        def h_step(t2, carry):
+        def h_pair(t2):
             at, ls = [], []
             for u in range(2):
                 t = base + jnp.minimum(2 * t2 + u, cnt - 1)
@@ -89,9 +89,13 @@
                         jnp.concatenate([spread(l, 2 * r, l, 2 * r + 1) for r in range(c, c + HN)], axis=0).astype(BF16)
                         for l in ls], axis=1)
                     hbuf[c:c + HN, t2] = pair(jnp.dot(w, rhs, preferred_element_type=F32))
+
+        def h_step(step, carry):
+            for u in range(HU):
+                h_pair(HU * step + u)
             return carry
 
-        lax.fori_loop(0, (cnt + 1) // 2, h_step, 0)
+        lax.fori_loop(0, (cnt + 2 * HU - 1) // (2 * HU), h_step, 0)
         depth, first = (3, 6) if half else (6, 0)
 
         def chunk(n, k0):
@@ -110,16 +114,16 @@
 
             @pl.when(longest > CHUNK)
             def _():
-                def again(n, carry):
+                def more(n, carry):
                     s0, s1 = meta[0, n], meta[0, n + 1]
 
                     def c_step(c, carry):
-                        chunk(n, s0 + CHUNK * c)
+                        chunk(n, jnp.minimum(s0 + CHUNK * c, s1 - CHUNK))
                         return carry
 
-                    return lax.fori_loop(0, (s1 - s0 + CHUNK - 1) // CHUNK, c_step, carry)
-
-                lax.fori_loop(NB * i, NB * i + NB, again, 0)
+                    return lax.fori_loop(1, (s1 - s0 + CHUNK - 1) // CHUNK, c_step, carry)
+
+                lax.fori_loop(NB * i, NB * i + NB, more, 0)
             return carry
 
         lax.fori_loop(0, 32 // NB, n_step, 0)
@@ -127,7 +131,7 @@
         for k in range(8):
             o = obuf[256 * k:256 * k + 256, :]
             high = o.astype(BF16)
-            s = sbuf[:, 256 * k:256 * k + 256]
+            s = sig[:, 256 * k:256 * k + 256]
             r += jnp.dot(s, high, preferred_element_type=F32)
         r = jnp.where(iota((256, 256), 1) < 8 * cnt, r, 0.0)
         e = ebuf[...].astype(BF16)
@@ -156,7 +160,6 @@
             pltpu.VMEM((256 + CHUNK, 9, 8, 128), F32),
             pltpu.VMEM((192, GROUP // 2, 16, 128), BF16),
             pltpu.VMEM(((256 + CHUNK) * 8, 256), F32),
-            pltpu.VMEM((256, 2048), BF16),
             pltpu.VMEM((256, 256), F32),
             pltpu.VMEM((256, 256), F32),
         ],
@@ -222,7 +225,8 @@
     sig_at = iota((256, 2048), 1)
     where = jnp.sum(jnp.where(by_n == sig_at // 8, first.astype(F32), 0.0), axis=0, keepdims=True).astype(I32)
     inner = iota((1, 2048), 1) % 8
-    sig[...] = jnp.where(inner < 6, 6 * where + inner, -1)
+    target = jnp.where(inner < 6, 6 * where + inner, -1)
+    sig[...] = (iota((256, 2048), 0) == target).astype(F32).astype(BF16)
     other = across(q)
     within = lanes((other == q) & (wide < g))
     chunks_row = (rows(q == lane) + 7) // 8
@@ -433,7 +437,7 @@
             jax.ShapeDtypeStruct((1, 512), I32),
             jax.ShapeDtypeStruct((1, 256), I32),
             jax.ShapeDtypeStruct((1, 128), I32),
-            jax.ShapeDtypeStruct((1, 2048), I32),
+            jax.ShapeDtypeStruct((256, 2048), BF16),
         ],
         in_specs=[hbm, smem, smem, hbm, hbm],
         out_specs=[vmem] * 8,

time: 76.8 us -> 67.4 us (0.88)
  Pallas kernels: 76 us -> 66.7 us
    pallas_call x1, Pallas kernels: 23.7 us -> 15.8 us  [reduce(): pl.pallas_call(reduce_kernel, out_shape=jax.ShapeDtypeStruct((2, 8, 128),...]
    pallas_call x1, Pallas kernels: 19.7 us -> 18.2 us  [contract(): pl.pallas_call(contract_kernel, out_shape=jax.ShapeDtypeStruct((256, 256)...]
where the time goes in v8:
time: 67.4 us; the launch traced here: 67.3 us
  Pallas kernels  66.7 us (99%)
    pallas_call x1, Pallas kernels, gather(): pl.pallas_call(gather_kernel, out_shape=[jax.ShapeDtypeStruct((2, 4, 4, 3...  32.6 us
    pallas_call x1, Pallas kernels, contract(): pl.pallas_call(contract_kernel, out_shape=jax.ShapeDtypeStruct((256, 256)...  18.2 us
    pallas_call x1, Pallas kernels, reduce(): pl.pallas_call(reduce_kernel, out_shape=jax.ShapeDtypeStruct((2, 8, 128),...  15.8 us

profile of v8, /device:TPU:1, one launch (start us, length us, event | category | flops | bytes accessed | tf_op | source)
XLA Modules:
  0.0 67.3 jit_solution(6180874970715704524)
XLA Ops:
  0.0 32.6 %gather.1 = (bf16[2,4,4,384,128]{4,3,2,1,0:T(8,128)(2,1)S(1)}, bf16[2,4,4,384,128]{4,3,2,1,0:T(8,128)(2,1)S(1)}, bf16[12,128,256]{2,1,0:T(8,128)(2,1)S(1)}, f32[...) custom-call(bf16[288,128]{1,0:T(8,128)(2,1)} %bitcast.12, ...), custom_call_target="tpu_custom_call" | custom-call | tf_op jit(solution)/shard_map/gather/pallas_call | solution.py:430
  32.6 18.2 %contract.1 = bf16[256,256]{1,0:T(8,128)(2,1)S(1)} custom-call(s32[1,512]{1,0:T(1,128)S(1)} %get-tuple-element.13.codex, s32[1,256]{1,0:T(1,128)S(1)} %get-tuple-element.14.codep, s32[1,128]{1,0:T(1,128)S(1)} %get-tuple-element.15.meta, bf16[256,2048]{1,0:T(8,128)(2,1)S(1)} %get-tuple-element.16.sig, bf16[256,48,128]{2,1,0:T(8,128)(2,1)S(1)} %bitcast.9, ...), custom_call_target="tpu_custom_call" | custom-call | tf_op jit(solution)/shard_map/contract/pallas_call | solution.py:154
  50.9 15.8 %reduce.1 = f32[2,8,128]{2,1,0:T(8,128)S(1)} custom-call(bf16[4,8,8,256]{3,2,1,0:T(8,128)(2,1)S(1)} %bitcast.11), custom_call_target="tpu_custom_call" | custom-call | tf_op jit(solution)/shard_map/reduce/pallas_call | solution.py:508
  66.7 0.6 add_bitcast_fusion

commit v9 on v8

--- a/solution.py
+++ b/solution.py
@@ -12,9 +12,9 @@
 GROUP = 32
 CHUNK = 16
 XROWS = 44
-XUN = 4
+XUN = 11
 HN = 48
-NB = 16
+NB = 32
 HU = 2
 
 

time: 67.4 us -> 72.4 us (1.074)
  Pallas kernels: 66.7 us -> 71.7 us
    pallas_call x1, Pallas kernels: 15.8 us -> 19.3 us  [reduce(): pl.pallas_call(reduce_kernel, out_shape=jax.ShapeDtypeStruct((2, 8, 128),...]
    pallas_call x1, Pallas kernels: 18.2 us -> 19.7 us  [contract(): pl.pallas_call(contract_kernel, out_shape=jax.ShapeDtypeStruct((256, 256)...]
where the time goes in v9:
time: 72.4 us; the launch traced here: 72.3 us
  Pallas kernels  71.7 us (99%)
    pallas_call x1, Pallas kernels, gather(): pl.pallas_call(gather_kernel, out_shape=[jax.ShapeDtypeStruct((2, 4, 4, 3...  32.6 us
    pallas_call x1, Pallas kernels, contract(): pl.pallas_call(contract_kernel, out_shape=jax.ShapeDtypeStruct((256, 256)...  19.7 us
    pallas_call x1, Pallas kernels, reduce(): pl.pallas_call(reduce_kernel, out_shape=jax.ShapeDtypeStruct((2, 8, 128),...  19.3 us

profile of v9, /device:TPU:1, one launch (start us, length us, event | category | flops | bytes accessed | tf_op | source)
XLA Modules:
  0.0 72.3 jit_solution(6769319642834325654)
XLA Ops:
  0.0 32.6 %gather.1 = (bf16[2,4,4,384,128]{4,3,2,1,0:T(8,128)(2,1)S(1)}, bf16[2,4,4,384,128]{4,3,2,1,0:T(8,128)(2,1)S(1)}, bf16[12,128,256]{2,1,0:T(8,128)(2,1)S(1)}, f32[...) custom-call(bf16[288,128]{1,0:T(8,128)(2,1)} %bitcast.12, ...), custom_call_target="tpu_custom_call" | custom-call | tf_op jit(solution)/shard_map/gather/pallas_call | solution.py:430
  32.6 19.7 %contract.1 = bf16[256,256]{1,0:T(8,128)(2,1)S(1)} custom-call(s32[1,512]{1,0:T(1,128)S(1)} %get-tuple-element.13.codex, s32[1,256]{1,0:T(1,128)S(1)} %get-tuple-element.14.codep, s32[1,128]{1,0:T(1,128)S(1)} %get-tuple-element.15.meta, bf16[256,2048]{1,0:T(8,128)(2,1)S(1)} %get-tuple-element.16.sig, bf16[256,48,128]{2,1,0:T(8,128)(2,1)S(1)} %bitcast.9, ...), custom_call_target="tpu_custom_call" | custom-call | tf_op jit(solution)/shard_map/contract/pallas_call | solution.py:154
  52.4 19.3 %reduce.1 = f32[2,8,128]{2,1,0:T(8,128)S(1)} custom-call(bf16[4,8,8,256]{3,2,1,0:T(8,128)(2,1)S(1)} %bitcast.11), custom_call_target="tpu_custom_call" | custom-call | tf_op jit(solution)/shard_map/reduce/pallas_call | solution.py:508
  71.7 0.6 add_bitcast_fusion

commit v10 on v9

--- a/solution.py
+++ b/solution.py
@@ -98,46 +98,56 @@
         lax.fori_loop(0, (cnt + 2 * HU - 1) // (2 * HU), h_step, 0)
         depth, first = (3, 6) if half else (6, 0)
 
-        def chunk(n, k0):
-            xs = jnp.concatenate([xbuf[pl.ds(k0, CHUNK), first + j].reshape(CHUNK * 8, 128).astype(BF16) for j in range(depth)], axis=1)
-            hs = jnp.concatenate([hbuf[n * depth + j].reshape(GROUP * 8, 128) for j in range(depth)], axis=1)
-            o = lax.dot_general(xs, hs, NT, preferred_element_type=F32)
-            obuf[pl.ds(pl.multiple_of(8 * k0, 8), CHUNK * 8), :] = o
-
-        def n_step(i, carry):
-            ends = [meta[0, NB * i + u] for u in range(NB + 1)]
-            for u in range(NB):
-                chunk(NB * i + u, ends[u])
-            longest = ends[1] - ends[0]
-            for u in range(1, NB):
-                longest = jnp.maximum(longest, ends[u + 1] - ends[u])
-
-            @pl.when(longest > CHUNK)
-            def _():
-                def more(n, carry):
-                    s0, s1 = meta[0, n], meta[0, n + 1]
-
-                    def c_step(c, carry):
-                        chunk(n, jnp.minimum(s0 + CHUNK * c, s1 - CHUNK))
-                        return carry
-
-                    return lax.fori_loop(1, (s1 - s0 + CHUNK - 1) // CHUNK, c_step, carry)
-
-                lax.fori_loop(NB * i, NB * i + NB, more, 0)
-            return carry
-
-        lax.fori_loop(0, 32 // NB, n_step, 0)
-        r = jnp.zeros((256, 256), F32)
-        for k in range(8):
-            o = obuf[256 * k:256 * k + 256, :]
-            high = o.astype(BF16)
-            s = sig[:, 256 * k:256 * k + 256]
-            r += jnp.dot(s, high, preferred_element_type=F32)
-        r = jnp.where(iota((256, 256), 1) < 8 * cnt, r, 0.0)
-        e = ebuf[...].astype(BF16)
-        high = r.astype(BF16)
-        low = (r - high.astype(F32)).astype(BF16)
-        kbuf[...] += jnp.dot(high, e, preferred_element_type=F32) + jnp.dot(low, e, preferred_element_type=F32)
+        def finish(pairs):
+            lanes = max(pairs * 16, 128)
+            def chunk(n, k0):
+                xs = jnp.concatenate([xbuf[pl.ds(k0, CHUNK), first + j].reshape(CHUNK * 8, 128).astype(BF16) for j in range(depth)], axis=1)
+                hs = jnp.concatenate([hbuf[n * depth + j, 0:pairs].reshape(pairs * 16, 128) for j in range(depth)], axis=1)
+                o = lax.dot_general(xs, hs, NT, preferred_element_type=F32)
+                obuf[pl.ds(pl.multiple_of(8 * k0, 8), CHUNK * 8), 0:pairs * 16] = o
+
+            def n_step(i, carry):
+                ends = [meta[0, NB * i + u] for u in range(NB + 1)]
+                for u in range(NB):
+                    chunk(NB * i + u, ends[u])
+                longest = ends[1] - ends[0]
+                for u in range(1, NB):
+                    longest = jnp.maximum(longest, ends[u + 1] - ends[u])
+
+                @pl.when(longest > CHUNK)
+                def _():
+                    def more(n, carry):
+                        s0, s1 = meta[0, n], meta[0, n + 1]
+
+                        def c_step(c, carry):
+                            chunk(n, jnp.minimum(s0 + CHUNK * c, s1 - CHUNK))
+                            return carry
+
+                        return lax.fori_loop(1, (s1 - s0 + CHUNK - 1) // CHUNK, c_step, carry)
+
+                    lax.fori_loop(NB * i, NB * i + NB, more, 0)
+                return carry
+
+            lax.fori_loop(0, 32 // NB, n_step, 0)
+            r = jnp.zeros((256, lanes), F32)
+            for k in range(8):
+                o = obuf[256 * k:256 * k + 256, 0:lanes]
+                high = o.astype(BF16)
+                s = sig[:, 256 * k:256 * k + 256]
+                r += jnp.dot(s, high, preferred_element_type=F32)
+            r = jnp.where(iota((256, lanes), 1) < 8 * cnt, r, 0.0)
+            e = ebuf[0:lanes, :].astype(BF16)
+            high = r.astype(BF16)
+            low = (r - high.astype(F32)).astype(BF16)
+            kbuf[...] += jnp.dot(high, e, preferred_element_type=F32) + jnp.dot(low, e, preferred_element_type=F32)
+
+        @pl.when(cnt <= 8)
+        def _():
+            finish(4)
+
+        @pl.when(cnt > 8)
+        def _():
+            finish(GROUP // 2)
 
     for half, base, total in ((False, 0, nf), (True, nf, nh)):
         def g_step(g, carry, half=half, base=base, total=total):

time: 72.4 us -> 67.4 us (0.931); the launches traced: 72.3 us -> 68 us
  Pallas kernels: 71.7 us -> 67.4 us
    pallas_call x1, Pallas kernels: 19.3 us -> 16.8 us  [reduce(): pl.pallas_call(reduce_kernel, out_shape=jax.ShapeDtypeStruct((2, 8, 128),...]
    pallas_call x1, Pallas kernels: 19.7 us -> 18 us  [contract(): pl.pallas_call(contract_kernel, out_shape=jax.ShapeDtypeStruct((256, 256)...]
where the time goes in v10:
time: 67.4 us; the launch traced here: 68 us
  Pallas kernels  67.4 us (100%)
    pallas_call x1, Pallas kernels, gather(): pl.pallas_call(gather_kernel, out_shape=[jax.ShapeDtypeStruct((2, 4, 4, 3...  32.6 us
    pallas_call x1, Pallas kernels, contract(): pl.pallas_call(contract_kernel, out_shape=jax.ShapeDtypeStruct((256, 256)...  18 us
    pallas_call x1, Pallas kernels, reduce(): pl.pallas_call(reduce_kernel, out_shape=jax.ShapeDtypeStruct((2, 8, 128),...  16.8 us

profile of v10, /device:TPU:1, one launch (start us, length us, event | category | flops | bytes accessed | tf_op | source)
XLA Modules:
  0.0 68.0 jit_solution(6785694221313255595)
XLA Ops:
  0.0 32.6 %gather.1 = (bf16[2,4,4,384,128]{4,3,2,1,0:T(8,128)(2,1)S(1)}, bf16[2,4,4,384,128]{4,3,2,1,0:T(8,128)(2,1)S(1)}, bf16[12,128,256]{2,1,0:T(8,128)(2,1)S(1)}, f32[...) custom-call(bf16[288,128]{1,0:T(8,128)(2,1)} %bitcast.12, ...), custom_call_target="tpu_custom_call" | custom-call | tf_op jit(solution)/shard_map/gather/pallas_call | solution.py:440
  32.6 18.0 %contract.1 = bf16[256,256]{1,0:T(8,128)(2,1)S(1)} custom-call(s32[1,512]{1,0:T(1,128)S(1)} %get-tuple-element.13.codex, s32[1,256]{1,0:T(1,128)S(1)} %get-tuple-element.14.codep, s32[1,128]{1,0:T(1,128)S(1)} %get-tuple-element.15.meta, bf16[256,2048]{1,0:T(8,128)(2,1)S(1)} %get-tuple-element.16.sig, bf16[256,48,128]{2,1,0:T(8,128)(2,1)S(1)} %bitcast.9, ...), custom_call_target="tpu_custom_call" | custom-call | tf_op jit(solution)/shard_map/contract/pallas_call | solution.py:164
  50.6 16.8 %reduce.1 = f32[2,8,128]{2,1,0:T(8,128)S(1)} custom-call(bf16[4,8,8,256]{3,2,1,0:T(8,128)(2,1)S(1)} %bitcast.11), custom_call_target="tpu_custom_call" | custom-call | tf_op jit(solution)/shard_map/reduce/pallas_call | solution.py:518
  67.5 0.6 add_bitcast_fusion
